TPU v7x, 512 devices: a whole 4x4x16 slice. The times are simulated.
512 devices in a mesh: docs: 64 (over x, z_lo, core), blk: 8 (over y, z_hi).
Axes of the slice: x: 4, y: 4, z: 16 (z_hi: 2, z_lo: 8; z = z_hi * 8 + z_lo), core: 2. Of those that a mesh axis runs over, the one named last changes fastest.
Arguments:
- group_rows: bfloat16 [8, 16384, 2048], P('blk', 'docs'), may hold values from -0.14941406 to 0.14941406
- group_owner: int32 [8, 16384, 1], P('blk', 'docs'), may hold values from 0 to 63; in each aligned block of 256 rows (0 to 255, 256 to 511, ..., all dimensions but the last counted through in order) at most 8 rows name the same one
- group_doc: int32 [8, 16384], P('blk', 'docs'), may hold values from 0 to 255
- doc_weight: float32 [8, 16384], P('blk', 'docs'), may hold values from 0.1 to 1
- queries: bfloat16 [256, 2048], P('blk'), may hold values from -6 to 6
- precond: bfloat16 [2048, 2048], P(None, 'docs'), may hold values from -0.125 to 0.125
Outputs:
- scores: float32 [256, 8, 16384], P(None, 'blk', 'docs')
Inputs may be any that keep to these rules, and one draw needn't show every extreme that they name: `group_owner`: within the rows of one device, at most 8 groups name the same owner, and some owner gets exactly 8.
All inputs are finite; a program needn't handle non-finite values.
Results may differ from a plain program's by a relative error of at most 0.006.
Values may be sent and summed in bfloat16 or wider, within the bound.
A program may use at most 64 MiB of HBM per device.

v0:
```python
import jax
import jax.numpy as jnp
from jax import lax
from jax.sharding import PartitionSpec as P


def against_docs(left, high_part, low_part, weight):
    dims = (((1,), (1,)), ((), ()))
    product = lax.dot_general(left, high_part, dims, preferred_element_type=jnp.float32)
    product = product + lax.dot_general(left, low_part, dims, preferred_element_type=jnp.float32)
    return product * weight[None, :]


def shards(group_rows, group_owner, group_doc, doc_weight, queries, precond):
    rows = group_rows[0]
    owner = group_owner[0, :, 0]
    doc_index = group_doc[0]
    peers = lax.axis_size("docs")
    count = rows.shape[0]
    width = rows.shape[1]
    capacity = 2 * count // peers
    peer_ids = jnp.arange(peers, dtype=jnp.int32)
    owner_table = (owner[:, None] == peer_ids[None, :]).astype(jnp.int32)
    earlier = jnp.cumsum(owner_table, axis=0) - owner_table
    slot = jnp.sum(earlier * owner_table, axis=1)
    send_ids = jnp.full((peers, capacity), -1, jnp.int32).at[owner, slot].set(doc_index)
    doc_count = doc_weight.shape[1]
    doc_ids = jnp.arange(doc_count, dtype=jnp.int32)
    weight = doc_weight[0]
    query_pre = jnp.dot(queries, precond, preferred_element_type=jnp.float32).astype(jnp.bfloat16)
    send_rows = jnp.zeros((peers, capacity, width), jnp.bfloat16).at[owner, slot].set(rows)
    got_rows, got_ids = (
        lax.all_to_all(send_rows, "docs", split_axis=0, concat_axis=0, tiled=True),
        lax.all_to_all(send_ids, "docs", split_axis=0, concat_axis=0, tiled=True),
    )
    got_rows = got_rows.reshape(peers * capacity, width)
    got_ids = got_ids.reshape(peers * capacity)
    member_table = (doc_ids[:, None] == got_ids[None, :]).astype(jnp.bfloat16)
    doc_print = jnp.dot(member_table, got_rows, preferred_element_type=jnp.float32)
    high_part = doc_print.astype(jnp.bfloat16)
    low_part = (doc_print - high_part.astype(jnp.float32)).astype(jnp.bfloat16)
    full_rows = lax.all_gather(query_pre, "docs", axis=1, tiled=True)
    scores = against_docs(
        lax.all_gather(full_rows, "blk", axis=0, tiled=True), high_part, low_part, weight
    )
    return scores[:, None, :]


def solution(mesh):
    return jax.shard_map(
        shards,
        mesh=mesh,
        in_specs=(
            P("blk", "docs", None),
            P("blk", "docs", None),
            P("blk", "docs"),
            P("blk", "docs"),
            P("blk", None),
            P(None, "docs"),
        ),
        out_specs=P(None, "blk", "docs"),
        check_vma=False,
    )
```

profile of v0, /device:TPU:1, one launch (start us, length us, event | category | flops | bytes accessed | tf_op | source)
XLA Modules:
  0.0 392.1 jit_solution(211520665865208457)
XLA Ops:
  6.5 0.0 copy-start
  6.5 0.7 fusion.11
  7.3 0.6 reduce-window.6
  7.9 0.2 slice_reduce_fusion
  8.1 0.8 fusion.10
  8.9 0.7 or_select_fusion
  9.6 0.0 copy-start.2
  9.6 21.2 %scatter_fusion = s32[64,8]{0,1:T(8,128)S(1)} fusion(s32[64,8]{0,1:T(8,128)S(1)} %broadcast_in_dim.6, s32[256]{0:T(256)S(1)} %bitcast.39, s32[256]{0:T(256)} %bitcast.45), kind=kCustom, calls=%fused_computation | custom fusion | bytes 5120 | tf_op jit(solution)/shard_map/scatter | solution.py:26
  30.8 0.7 copy.18
  31.5 17.0 %all-to-all-start = ((s32[64,1,8]{2,1,0:T(1,128)}), s32[64,1,8]{2,1,0:T(1,128)S(1)}, u32[]{:S(2)}, u32[]{:S(2)}) async-start(s32[64,1,8]{2,1,0:T(1,128)} %copy.18), calls=%async_computation | async-start | bytes 65536 | tf_op jit(solution)/shard_map/all_to_all | solution.py:34
  48.6 1.6 broadcast_in_dim.7
  50.1 0.0 copy-done.2
  50.1 44.3 %scatter_fusion.1 = bf16[64,8,2048]{2,1,0:T(8,128)(2,1)} fusion(bf16[64,8,2048]{2,1,0:T(8,128)(2,1)} %broadcast_in_dim.7, s32[256]{0:T(256)S(1)} %bitcast.40, bf16[256,2048]{1,0:T(8,128)(2,1)S(1)} %bitcast.41), kind=kCustom, calls=%fused_computation.1 | custom fusion | bytes 3147776 | tf_op jit(solution)/shard_map/scatter | solution.py:31
  94.5 0.0 copy-start.3
  94.5 0.0 all-to-all-done
  94.5 13.4 %all-to-all-start.1 = ((bf16[64,8,2048]{2,1,0:T(8,128)(2,1)}), bf16[64,8,2048]{2,1,0:T(8,128)(2,1)}, u32[]{:S(2)}, u32[]{:S(2)}) async-start(bf16[64,8,2048]{2,1,0:T(8,128)(2,1)} %scatter_fusion.1), calls=%async_computation.1 | async-start | bytes 4194304 | tf_op jit(solution)/shard_map/all_to_all | solution.py:33
  107.9 0.0 all-gather.2.cloned.1.call-start
  108.0 0.0 copy-done
  108.0 0.0 copy-done.3
  108.0 0.2 convolution_convert_fusion
  108.1 0.1 copy.15
  108.2 188.9 %all_gather.6 = bf16[32,2048]{0,1:T(8,128)(2,1)S(1)} all-gather(bf16[32,32]{0,1:T(8,128)(2,1)S(1)} %copy.15), channel_id=1, replica_groups=mesh['docs'=64,'blk'=8] {'docs'}, dimensions={1}, use_global_device_ids=true | all-gather | bytes 133120 | tf_op jit(solution)/shard_map/all_gather | solution.py:42
  297.1 0.8 copy.16
  297.9 0.0 all-gather.2.cloned.1.call-update
  298.0 0.5 broadcast.101
  298.5 0.7 reduce.5
  299.2 0.1 eq.49
  299.3 0.0 all-to-all-done.1
  299.3 2.3 fusion
  301.6 0.0 copy-start.4
  301.6 80.4 %all-gather.2.cloned.1.call-done = bf16[256,2048]{1,0:T(8,128)(2,1)} async-done(((bf16[32,2048]{1,0:T(8,128)(2,1)}), bf16[256,2048]{1,0:T(8,128)(2,1)}) %all-gather.2.cloned.1.call-update) | async-done | bytes 1048592 | tf_op jit(solution)/shard_map/all_gather | solution.py:44
  382.0 0.0 copy-start.1
  382.0 1.8 fusion.5
  383.8 0.0 copy-done.4
  383.8 0.0 copy-done.1
  383.8 0.5 fusion.3
  384.3 1.0 copy.19
  (3 shorter events, 0.0 us)
Async XLA Ops:
  6.5 101.4 %copy-start = (bf16[32,2048]{1,0:T(8,128)(2,1)S(1)}, bf16[32,2048]{1,0:T(8,128)(2,1)}, u32[]{:S(2)}) copy-start(bf16[32,2048]{1,0:T(8,128)(2,1)} %param.10) | copy-start | bytes 393220
  9.6 40.6 %copy-start.2 = (bf16[1,256,2048]{2,1,0:T(8,128)(2,1)S(1)}, bf16[1,256,2048]{2,1,0:T(8,128)(2,1)}, u32[]{:S(2)}) copy-start(bf16[1,256,2048]{2,1,0:T(8,128)(2,1)} %param.6) | copy-start | bytes 3145732
  31.5 62.9 %all-to-all-start = ((s32[64,1,8]{2,1,0:T(1,128)}), s32[64,1,8]{2,1,0:T(1,128)S(1)}, u32[]{:S(2)}, u32[]{:S(2)}) async-start(s32[64,1,8]{2,1,0:T(1,128)} %copy.18), calls=%async_computation | async-start | bytes 65536 | tf_op jit(solution)/shard_map/all_to_all | solution.py:34
  94.5 13.5 %copy-start.3 = (bf16[2048,32]{0,1:T(8,128)(2,1)S(1)}, bf16[2048,32]{0,1:T(8,128)(2,1)}, u32[]{:S(2)}) copy-start(bf16[2048,32]{0,1:T(8,128)(2,1)} %param.11) | copy-start | bytes 393220
  94.5 204.8 %all-to-all-start.1 = ((bf16[64,8,2048]{2,1,0:T(8,128)(2,1)}), bf16[64,8,2048]{2,1,0:T(8,128)(2,1)}, u32[]{:S(2)}, u32[]{:S(2)}) async-start(bf16[64,8,2048]{2,1,0:T(8,128)(2,1)} %scatter_fusion.1), calls=%async_computation.1 | async-start | bytes 4194304 | tf_op jit(solution)/shard_map/all_to_all | solution.py:33
  107.9 274.1 %all-gather.2.cloned.1.call-start = ((), (), s32[]{:S(2)}) async-start(), calls=%async_computation.2 | async-start | bytes 1179648 | tf_op jit(solution)/shard_map/all_gather | solution.py:44
  301.6 82.2 %copy-start.4 = (f32[1,256]{1,0:T(1,128)S(1)}, f32[1,256]{1,0:T(1,128)}, u32[]{:S(2)}) copy-start(f32[1,256]{1,0:T(1,128)} %param.9) | copy-start | bytes 3076
  382.0 1.8 copy-start.1
Sparse Core Ops, SparseCore 0:
  298.1 83.8 all-gather.1
where the time goes:
time: 395 us; the launch traced here: 392 us
  blocking collectives  189 us (48%)
  waiting for transfers between devices  80.4 us (20%)
  local copies, waits for them, and re-layouts  70.6 us (18%)
  starting transfers between devices  30.5 us (8%)
  between operations  13.5 us (3%)
  matrix products  4.72 us (1%)
    all_gather x1, blocking collectives, shards(): full_rows = lax.all_gather(query_pre, 'docs', axis=1, tiled=True)  189 us
    all_gather x1, waiting for transfers between devices, shards(): lax.all_gather(full_rows, 'blk', axis=0, tiled=True)  80.4 us
    scatter x1, local copies, waits for them, and re-layouts, shards(): jnp.zeros((peers, capacity, width), jnp.bfloat16).at[owner, slot].set(rows)  44.3 us
    scatter x1, local copies, waits for them, and re-layouts, shards(): jnp.full((peers, capacity), -1, jnp.int32).at[owner, slot].set(doc_index)  21.2 us
    all_to_all x1, starting transfers between devices, shards(): lax.all_to_all(send_ids, 'docs', split_axis=0, concat_axis=0, tiled=True)  17 us
    all_to_all x1, starting transfers between devices, shards(): lax.all_to_all(send_rows, 'docs', split_axis=0, concat_axis=0, tiled=True)  13.4 us
  transfers between devices with their start and end apart: 3, of which 1 were waited for; matrix products, arithmetic and copies ran while one was open for 13% of the time, Pallas kernels for 0%

commit v1 on v0

v1 whole, which is shorter than its diff:
```python
import jax
import jax.numpy as jnp
from jax import lax
from jax.sharding import PartitionSpec as P

NT = (((1,), (1,)), ((), ()))


def shards(group_rows, group_owner, group_doc, doc_weight, queries, precond):
    rows = group_rows[0]
    owner = group_owner[0, :, 0]
    doc_index = group_doc[0]
    peers = lax.axis_size("docs")
    count = rows.shape[0]
    capacity = 2 * count // peers
    slots = peers * capacity
    peer_ids = jnp.arange(peers, dtype=jnp.int32)
    owner_table = (peer_ids[:, None] == owner[None, :])
    order = jnp.arange(count, dtype=jnp.int32)
    before = (order[:, None] < order[None, :]).astype(jnp.bfloat16)
    earlier = jnp.dot(owner_table.astype(jnp.bfloat16), before, preferred_element_type=jnp.float32)
    rank = jnp.sum(jnp.where(owner_table, earlier, 0.0), axis=0).astype(jnp.int32)
    slot = owner * capacity + rank
    pick = jnp.arange(slots, dtype=jnp.int32)[:, None] == slot[None, :]
    send_ids = jnp.max(jnp.where(pick, doc_index[None, :], -1), axis=1).reshape(peers, capacity)
    got_ids = lax.all_to_all(send_ids, "docs", split_axis=0, concat_axis=0, tiled=True).reshape(slots)
    query_pre = jnp.dot(queries, precond, preferred_element_type=jnp.float32).astype(jnp.bfloat16)
    full_rows = lax.all_gather(query_pre, "docs", axis=1, tiled=True)
    full = lax.all_gather(full_rows, "blk", axis=0, tiled=True)
    part = lax.dot_general(rows, full, NT, preferred_element_type=jnp.float32).astype(jnp.bfloat16)
    send = jnp.dot(pick.astype(jnp.bfloat16), part, preferred_element_type=jnp.float32).astype(jnp.bfloat16)
    send = send.reshape(peers, capacity, send.shape[1])
    got = lax.all_to_all(send, "docs", split_axis=0, concat_axis=0, tiled=True)
    got = got.reshape(slots, got.shape[2])
    doc_ids = jnp.arange(doc_weight.shape[1], dtype=jnp.int32)
    member = (got_ids[:, None] == doc_ids[None, :]).astype(jnp.bfloat16)
    scores = lax.dot_general(got, member, (((0,), (0,)), ((), ())), preferred_element_type=jnp.float32)
    return (scores * doc_weight[0][None, :])[:, None, :]


def solution(mesh):
    return jax.shard_map(
        shards,
        mesh=mesh,
        in_specs=(
            P("blk", "docs", None),
            P("blk", "docs", None),
            P("blk", "docs"),
            P("blk", "docs"),
            P("blk", None),
            P(None, "docs"),
        ),
        out_specs=P(None, "blk", "docs"),
        check_vma=False,
    )
```

time: 395 us -> 259 us (0.66)
  local copies, waits for them, and re-layouts: 70.6 us -> 4.65 us
  blocking collectives: 189 us -> 129 us
  starting transfers between devices: 30.5 us -> 11.4 us
  waiting for transfers between devices: 80.4 us -> 95.3 us
    scatter x2 -> x0, local copies, waits for them, and re-layouts: 65.6 us -> none  [the longest x1 44.3 us: shards(): jnp.zeros((peers, capacity, width), jnp.bfloat16).at[owner, slot].set(rows)]
    all_gather x1, blocking collectives: 189 us -> 129 us  [shards(): full_rows = lax.all_gather(query_pre, 'docs', axis=1, tiled=True)]
    all_to_all x1, waiting for transfers between devices: 0.01 us -> 17.9 us  [shards(): got = lax.all_to_all(send, 'docs', split_axis=0, concat_axis=0, tiled=True)]
    all_to_all x1, starting transfers between devices: 17 us -> 4.2 us  [shards(): lax.all_to_all(send_ids, 'docs', split_axis=0, concat_axis=0, tiled=True)]
    all_to_all x1, starting transfers between devices: 13.4 us -> 7.2 us  [shards(): got = lax.all_to_all(send, 'docs', split_axis=0, concat_axis=0, tiled=True)]
  transfers between devices with their start and end apart: 3 -> 3, of which waited for: 1 -> 2; matrix products, arithmetic and copies ran while one was open for 13% -> 2% of each run, Pallas kernels for 0% -> 0%
where the time goes in v1:
time: 259 us
  blocking collectives  129 us (50%)
  waiting for transfers between devices  95.3 us (37%)
  between operations  13.5 us (5%)
  starting transfers between devices  11.4 us (4%)
  local copies, waits for them, and re-layouts  4.65 us (2%)
  matrix products  4.45 us (2%)
    all_gather x1, blocking collectives, shards(): full_rows = lax.all_gather(query_pre, 'docs', axis=1, tiled=True)  129 us
    all_gather x1, waiting for transfers between devices, shards(): full = lax.all_gather(full_rows, 'blk', axis=0, tiled=True)  77.4 us
    all_to_all x1, waiting for transfers between devices, shards(): got = lax.all_to_all(send, 'docs', split_axis=0, concat_axis=0, tiled=True)  17.9 us
    all_to_all x1, starting transfers between devices, shards(): got = lax.all_to_all(send, 'docs', split_axis=0, concat_axis=0, tiled=True)  7.2 us
  transfers between devices with their start and end apart: 3, of which 2 were waited for; matrix products, arithmetic and copies ran while one was open for 2% of the time, Pallas kernels for 0%

profile of v1, /device:TPU:1, one launch (start us, length us, event | category | flops | bytes accessed | tf_op | source)
XLA Modules:
  0.0 259.1 jit_solution(14440110676353129902)
XLA Ops:
  6.5 0.0 copy-start
  6.5 0.0 all-gather.2.cloned.1.call-start
  6.5 1.2 convolution_convert_fusion.2
  7.7 0.1 copy.16
  7.8 129.0 %all_gather.6 = bf16[32,2048]{0,1:T(8,128)(2,1)S(1)} all-gather(bf16[32,32]{0,1:T(8,128)(2,1)S(1)} %copy.16), channel_id=1, replica_groups=mesh['docs'=64,'blk'=8] {'docs'}, dimensions={1}, use_global_device_ids=true | all-gather | bytes 133120 | tf_op jit(solution)/shard_map/all_gather | solution.py:28
  136.8 0.8 copy.17
  137.6 0.0 all-gather.2.cloned.1.call-update
  137.7 0.0 copy-start.1
  137.7 0.7 copy-done.1
  138.4 0.2 fusion.2
  138.5 0.0 copy-start.2
  138.6 0.7 copy-done.2
  139.2 0.1 select_reduce_fusion
  139.4 0.7 all_to_all.10
  140.1 4.2 %all-to-all-start.1 = ((s32[64,1,8]{2,1,0:T(1,128)}), s32[64,1,8]{2,1,0:T(1,128)S(1)}, u32[]{:S(2)}, u32[]{:S(2)}) async-start(s32[64,1,8]{2,1,0:T(1,128)} %bitcast.5), calls=%async_computation.1 | async-start | bytes 65536 | tf_op jit(solution)/shard_map/all_to_all | solution.py:26
  144.3 77.4 %all-gather.2.cloned.1.call-done = bf16[256,2048]{1,0:T(8,128)(2,1)} async-done(((bf16[32,2048]{1,0:T(8,128)(2,1)}), bf16[256,2048]{1,0:T(8,128)(2,1)}) %all-gather.2.cloned.1.call-update) | async-done | bytes 1048592 | tf_op jit(solution)/shard_map/all_gather | solution.py:29
  221.7 0.0 copy-done
  221.7 2.7 %fusion.1 = bf16[64,8,256]{2,1,0:T(8,128)(2,1)} fusion(bf16[256,2048]{1,0:T(8,128)(2,1)} %all-gather.2.cloned.1.call-done, bf16[1,256,2048]{2,1,0:T(8,128)(2,1)S(1)} %copy-done, s32[256]{0:T(256)S(1)} %convert_add_fusion), kind=kOutput, calls=%fused_computation.3 | convolution fusion | flops 335872000 | bytes 2360320 | tf_op jit(solution)/shard_map/dot_general | solution.py:31
  224.4 0.0 all-to-all-done.1
  224.4 7.2 %all-to-all-start = ((bf16[64,8,256]{2,1,0:T(8,128)(2,1)}), bf16[64,8,256]{2,1,0:T(8,128)(2,1)S(1)}, u32[]{:S(2)}, u32[]{:S(2)}) async-start(bf16[64,8,256]{2,1,0:T(8,128)(2,1)} %fusion.1), calls=%async_computation | async-start | bytes 524288 | tf_op jit(solution)/shard_map/all_to_all | solution.py:33
  231.6 0.6 broadcast.7
  232.2 0.7 reduce.3
  232.9 0.1 eq.47
  233.0 0.0 copy-start.3
  233.0 17.9 %all-to-all-done = bf16[64,8,256]{2,1,0:T(8,128)(2,1)S(1)} async-done(((bf16[64,8,256]{2,1,0:T(8,128)(2,1)}), bf16[64,8,256]{2,1,0:T(8,128)(2,1)S(1)}, u32[]{:S(2)}, u32[]{:S(2)}) %all-to-all-start) | async-done | bytes 262176 | tf_op jit(solution)/shard_map/all_to_all | solution.py:33
  250.9 0.0 copy-done.3
  250.9 0.3 fusion
  251.2 1.0 copy.19
  (1 shorter events, 0.0 us)
Async XLA Ops:
  6.5 215.1 %copy-start = (bf16[1,256,2048]{2,1,0:T(8,128)(2,1)S(1)}, bf16[1,256,2048]{2,1,0:T(8,128)(2,1)}, u32[]{:S(2)}) copy-start(bf16[1,256,2048]{2,1,0:T(8,128)(2,1)} %param.6) | copy-start | bytes 3145732
  6.5 215.1 %all-gather.2.cloned.1.call-start = ((), (), s32[]{:S(2)}) async-start(), calls=%async_computation.2 | async-start | bytes 1179648 | tf_op jit(solution)/shard_map/all_gather | solution.py:29
  137.7 0.7 copy-start.1
  138.5 0.7 copy-start.2
  140.1 84.3 %all-to-all-start.1 = ((s32[64,1,8]{2,1,0:T(1,128)}), s32[64,1,8]{2,1,0:T(1,128)S(1)}, u32[]{:S(2)}, u32[]{:S(2)}) async-start(s32[64,1,8]{2,1,0:T(1,128)} %bitcast.5), calls=%async_computation.1 | async-start | bytes 65536 | tf_op jit(solution)/shard_map/all_to_all | solution.py:26
  224.4 26.5 %all-to-all-start = ((bf16[64,8,256]{2,1,0:T(8,128)(2,1)}), bf16[64,8,256]{2,1,0:T(8,128)(2,1)S(1)}, u32[]{:S(2)}, u32[]{:S(2)}) async-start(bf16[64,8,256]{2,1,0:T(8,128)(2,1)} %fusion.1), calls=%async_computation | async-start | bytes 524288 | tf_op jit(solution)/shard_map/all_to_all | solution.py:33
  233.0 17.9 %copy-start.3 = (f32[1,256]{1,0:T(1,128)S(1)}, f32[1,256]{1,0:T(1,128)}, u32[]{:S(2)}) copy-start(f32[1,256]{1,0:T(1,128)} %param.9) | copy-start | bytes 3076
Sparse Core Ops, SparseCore 0:
  137.8 83.8 all-gather.1

commit v2 on v1

v2 whole, which is shorter than its diff:
```python
import functools

import jax
import jax.numpy as jnp
from jax import lax
from jax.experimental import pallas as pl
from jax.experimental.pallas import tpu as pltpu
from jax.sharding import PartitionSpec as P

X, Y, Z_LO, Z_HI = 4, 4, 8, 2
MESH = pl.DeviceIdType.MESH
NT = (((1,), (1,)), ((), ()))
TN = (((0,), (0,)), ((), ()))
F32, BF16 = jnp.float32, jnp.bfloat16


def dot(a, b, dims):
    return lax.dot_general(a, b, dims, preferred_element_type=F32)


def iota(shape, axis):
    return lax.broadcasted_iota(jnp.int32, shape, axis)


def kernel(
    rows_hbm, owner_ref, doc_ref, query_hbm, pre_hbm, out_ref,
    rows, owner2, doc2, query, pre, half, swapped, ztile, gathered, pick,
    id_send, id_got, send, got, member, result,
    loc_sem, sw_s, sw_r, za_s, za_r, zb_s, zb_r, x_s, x_r, y_s, y_r,
    i_s, i_r, a_s, a_r, o_s, o_r,
):
    zn = Z_LO * Z_HI
    reach = zn // 4
    chips = X * Z_LO
    count = rows.shape[1]
    owners = 2 * chips
    cap = 2 * count // owners
    d, b = lax.axis_index("docs"), lax.axis_index("blk")
    core, chip = d % 2, d // 2
    x, z_lo = chip // Z_LO, chip % Z_LO
    y, z_hi = b // Z_HI, b % Z_HI
    z = z_hi * Z_LO + z_lo

    def at(dx=0, dy=0, dz=0, other=False):
        nx, ny, nz = (x + dx) % X, (y + dy) % Y, (z + dz + zn) % zn
        nc = 1 - core if other else core
        return {"docs": (nx * Z_LO + nz % Z_LO) * 2 + nc, "blk": ny * Z_HI + nz // Z_LO}

    def remote(src, dst, s, r, device):
        return pltpu.make_async_remote_copy(
            src_ref=src, dst_ref=dst, send_sem=s, recv_sem=r, device_id=device, device_id_type=MESH
        )

    load_query = pltpu.make_async_copy(query_hbm, query, loc_sem.at[0])
    load_pre = pltpu.make_async_copy(pre_hbm, pre, loc_sem.at[1])
    load_rows = pltpu.make_async_copy(rows_hbm, rows.at[0], loc_sem.at[2])
    load_query.start()
    load_pre.start()
    load_rows.start()

    partners = [at(other=True)]
    for j in range(1, reach + 1):
        partners += [at(dz=j), at(dz=-j)]
    partners += [at(dx=j) for j in range(1, X)] + [at(dy=j) for j in range(1, Y)]
    barrier = pltpu.get_barrier_semaphore()
    for device in partners:
        pl.semaphore_signal(barrier, inc=1, device_id=device, device_id_type=MESH)

    load_query.wait()
    load_pre.wait()
    wide = jnp.concatenate([pre[...]] * 4, axis=0)
    block = dot(query[...], wide, NT)
    keep = iota(block.shape, 1) // 32 == d % 4
    block = jnp.where(keep, block, 0.0).astype(BF16)
    half[...] = block.reshape(half.shape)

    pl.semaphore_wait(barrier, len(partners))

    swaps = [
        remote(half.at[1 - core], swapped, sw_s.at[0], sw_r.at[0], at(other=True)),
        remote(owner_ref, owner2, sw_s.at[1], sw_r.at[1], at(other=True)),
        remote(doc_ref, doc2, sw_s.at[2], sw_r.at[2], at(other=True)),
        remote(rows_hbm, rows.at[1], sw_s.at[3], sw_r.at[3], at(other=True)),
    ]
    for copy in swaps:
        copy.start()
    swaps[0].wait()
    ztile[z] = half[core] + swapped[...]
    own_tile = ztile.at[z]
    near = {}
    for j in range(reach, 0, -1):
        for k, dz in ((2 * j - 2, j), (2 * j - 1, -j)):
            near[dz] = remote(own_tile, own_tile, za_s.at[k], za_r.at[k], at(dz=dz))
            near[dz].start()

    swaps[1].wait()
    swaps[2].wait()
    slots = owners * 2 * cap
    before = (iota((count, count), 0) < iota((count, count), 1)).astype(BF16)
    id_table = jnp.zeros((chips, 128), F32)
    for side in range(2):
        owner_row = (owner_ref if side == 0 else owner2)[...]
        doc_row = (doc_ref if side == 0 else doc2)[...]
        table = iota((owners, count), 0) == owner_row
        earlier = dot(table.astype(BF16), before, (((1,), (0,)), ((), ())))
        rank = jnp.sum(jnp.where(table, earlier, 0.0), axis=0, keepdims=True).astype(jnp.int32)
        source = core if side == 0 else 1 - core
        lane = (owner_row % 2) * (2 * cap) + source * cap + rank
        to_chip = owner_row // 2
        slot = to_chip * (4 * cap) + lane
        pick[:, side * count:(side + 1) * count] = (iota((slots, count), 0) == slot).astype(BF16)
        doc_one = (doc_row + 1).astype(F32)
        chip_side = jnp.where(iota((chips, count), 0) == to_chip, doc_one, 0.0).astype(BF16)
        lane_side = (iota((128, count), 0) == lane).astype(BF16)
        id_table = id_table + dot(chip_side, lane_side, NT)
    id_send[...] = id_table.reshape(id_send.shape)

    far = []
    for j in range(1, reach + 1):
        for k, dz in ((2 * j - 2, j), (2 * j - 1, -j)):
            near[dz].wait_recv()
            if dz == -reach:
                continue
            tile = ztile.at[(z - dz + zn) % zn]
            copy = remote(tile, tile, zb_s.at[k], zb_r.at[k], at(dz=reach if dz > 0 else -reach))
            copy.start()
            far.append(copy)
    for copy in far:
        copy.wait_recv()

    for hi in range(Z_HI):
        for p in range(Z_LO // 2):
            first = hi * Z_LO + 2 * p
            gathered[y, x, hi * 16:(hi + 1) * 16, p * 128:(p + 1) * 128] = ztile[first] + ztile[first + 1]
    own_piece = gathered.at[y, x]
    across = []
    for j in range(1, X):
        copy = remote(own_piece, own_piece, x_s.at[j - 1], x_r.at[j - 1], at(dx=j))
        copy.start()
        across.append(copy)
    along = []
    for i in range(X):
        if i:
            across[i - 1].wait_recv()
        piece = gathered.at[y, (x - i + X) % X]
        for j in range(1, Y):
            copy = remote(piece, piece, y_s.at[j - 1, i], y_r.at[j - 1, i], at(dy=j))
            copy.start()
            along.append(copy)

    def to(i):
        other = (chip + i) % chips
        return other, {"docs": other * 2 + core, "blk": b}

    def id_copy(i):
        other, device = to(i)
        return remote(id_send.at[other], id_got.at[chip], i_s.at[i], i_r.at[i], device)

    def score_copy(i):
        other, device = to(i)
        return remote(send.at[other], got.at[chip], a_s.at[i], a_r.at[i], device)

    def each(fn):
        lax.fori_loop(1, chips, lambda i, c: (fn(i), c)[1], 0)

    each(lambda i: id_copy(i).start())
    own_ids = pltpu.make_async_copy(id_send.at[chip], id_got.at[chip], loc_sem.at[3])
    own_ids.start()
    load_rows.wait()
    swaps[3].wait()
    for copy in along:
        copy.wait_recv()

    part = None
    span = gathered.shape[3]
    for i in range(X):
        left = rows[:, :, i * span:(i + 1) * span].reshape(2 * count, span)
        right = gathered[:, i].reshape(Y * gathered.shape[2], span)
        term = dot(left, right, NT)
        part = term if part is None else part + term
    packed = dot(pick[...], part.astype(BF16), (((1,), (0,)), ((), ()))).astype(BF16)
    send[...] = packed.reshape(send.shape)

    each(lambda i: score_copy(i).start())
    own_scores = pltpu.make_async_copy(send.at[chip], got.at[chip], loc_sem.at[4])
    own_scores.start()

    own_ids.wait()
    each(lambda i: id_copy(i).wait_recv())
    per = chips * 2 * cap
    spread = (iota((per, chips), 0) // (2 * cap) == iota((per, chips), 1)).astype(BF16)
    ids = dot(spread, id_got[...].reshape(chips, 128).astype(BF16), (((1,), (0,)), ((), ())))
    for e in range(2):
        mine = iota(ids.shape, 1) == e * 2 * cap + iota(ids.shape, 0) % (2 * cap)
        column = jnp.sum(jnp.where(mine, ids, 0.0), axis=1, keepdims=True).astype(jnp.int32) - 1
        member[e] = (column == iota((per, member.shape[2]), 1)).astype(BF16)

    own_scores.wait()
    each(lambda i: score_copy(i).wait_recv())
    for e in (1 - core, core):
        total = dot(got[:, e].reshape(per, got.shape[3]), member[e], TN)
        shape = (out_ref.shape[0],) + out_ref.shape[2:]
        if e is core:
            out_ref[:, core] = total.reshape(shape)
        else:
            result[...] = total.reshape(shape)
            give = remote(result, out_ref.at[:, core], o_s, o_r, at(other=True))
            give.start()
    give.wait()

    for copy in list(near.values()) + far + across + along:
        copy.wait_send()
    each(lambda i: id_copy(i).wait_send())
    each(lambda i: score_copy(i).wait_send())


def shards(group_rows, group_owner, group_doc, doc_weight, queries, precond):
    rows = group_rows[0]
    count, width = rows.shape
    docs, blks = lax.axis_size("docs"), lax.axis_size("blk")
    chips, zn = X * Z_LO, Z_LO * Z_HI
    reach = zn // 4
    cap = 2 * count // docs
    own_q, part = queries.shape[0], precond.shape[1]
    doc_count = doc_weight.shape[1]
    lanes = Y * Z_HI * own_q // 2
    dma = pltpu.SemaphoreType.DMA
    any_spec = pl.BlockSpec(memory_space=pl.ANY)
    vmem = pl.BlockSpec(memory_space=pltpu.VMEM)
    total = pl.pallas_call(
        kernel,
        out_shape=jax.ShapeDtypeStruct((blks, 2, own_q // 2, doc_count), F32),
        in_specs=[any_spec, vmem, vmem, any_spec, any_spec],
        out_specs=vmem,
        scratch_shapes=[
            pltpu.VMEM((2, count, width), BF16),
            pltpu.VMEM((1, count), jnp.int32),
            pltpu.VMEM((1, count), jnp.int32),
            pltpu.VMEM(queries.shape, BF16),
            pltpu.VMEM((part, width), BF16),
            pltpu.VMEM((2, own_q // 2, 128), BF16),
            pltpu.VMEM((own_q // 2, 128), BF16),
            pltpu.VMEM((zn, own_q // 2, 128), BF16),
            pltpu.VMEM((Y, X, Z_HI * own_q // 2, width // X), BF16),
            pltpu.VMEM((docs * 2 * cap, 2 * count), BF16),
            pltpu.VMEM((chips, 1, 128), F32),
            pltpu.VMEM((chips, 1, 128), F32),
            pltpu.VMEM((chips, 2, 2 * cap, lanes), BF16),
            pltpu.VMEM((chips, 2, 2 * cap, lanes), BF16),
            pltpu.VMEM((2, chips * 2 * cap, doc_count), BF16),
            pltpu.VMEM((blks, own_q // 2, doc_count), F32),
            dma((5,)), dma((4,)), dma((4,)),
            dma((2 * reach,)), dma((2 * reach,)), dma((2 * reach,)), dma((2 * reach,)),
            dma((max(X - 1, 1),)), dma((max(X - 1, 1),)),
            dma((max(Y - 1, 1), X)), dma((max(Y - 1, 1), X)),
            dma((chips,)), dma((chips,)), dma((chips,)), dma((chips,)),
            dma, dma,
        ],
        compiler_params=pltpu.CompilerParams(collective_id=0, has_side_effects=True),
    )(rows, group_owner.reshape(1, count), group_doc, queries, precond.T)
    scores = total.reshape(blks * own_q, doc_count) * doc_weight[0][None, :]
    return scores[:, None, :]


def solution(mesh):
    return jax.shard_map(
        shards,
        mesh=mesh,
        in_specs=(
            P("blk", "docs", None),
            P("blk", "docs", None),
            P("blk", "docs"),
            P("blk", "docs"),
            P("blk", None),
            P(None, "docs"),
        ),
        out_specs=P(None, "blk", "docs"),
        check_vma=False,
    )
```

time: 259 us -> 56.8 us (0.22)
  blocking collectives: 129 us -> 0 us
  waiting for transfers between devices: 95.3 us -> 0 us
  Pallas kernels: 0 us -> 54 us
  between operations: 13.5 us -> 0.02 us
  starting transfers between devices: 11.4 us -> 0 us
  matrix products: 4.45 us -> 0 us
  local copies, waits for them, and re-layouts: 4.65 us -> 0.67 us
    all_gather x1 -> x0, blocking collectives: 129 us -> none  [shards(): full_rows = lax.all_gather(query_pre, 'docs', axis=1, tiled=True)]
    all_gather x1 -> x0, waiting for transfers between devices: 77.4 us -> none  [shards(): full = lax.all_gather(full_rows, 'blk', axis=0, tiled=True)]
    pallas_call x0 -> x1, Pallas kernels: none -> 54 us  [shards(): pl.pallas_call(kernel, out_shape=jax.ShapeDtypeStruct((blks, 2, own_q //...]
    all_to_all x2 -> x0, waiting for transfers between devices: 17.9 us -> none  [the longest x1 17.9 us: shards(): got = lax.all_to_all(send, 'docs', split_axis=0, concat_axis=0, tiled=True)]
    all_to_all x2 -> x0, starting transfers between devices: 11.4 us -> none  [the longest x1 7.2 us: shards(): got = lax.all_to_all(send, 'docs', split_axis=0, concat_axis=0, tiled=True)]
    dot_general x4 -> x0, matrix products: 4.45 us -> none  [the longest x1 2.72 us: shards(): jnp.dot(pick.astype(jnp.bfloat16), part, preferred_element_type=jnp.float32)]
  transfers between devices with their start and end apart: 3 -> 0, of which waited for: 2 -> 0; matrix products, arithmetic and copies ran while one was open for 2% -> 0% of each run, Pallas kernels for 0% -> 0%
where the time goes in v2:
time: 56.8 us; the launch traced here: 56.6 us
  Pallas kernels  54 us (95%)
  other arithmetic  1.92 us (3%)
  local copies, waits for them, and re-layouts  0.67 us (1%)
    pallas_call x1, Pallas kernels, shards(): pl.pallas_call(kernel, out_shape=jax.ShapeDtypeStruct((blks, 2, own_q //...  54 us
    mul x1, other arithmetic, shards(): scores = total.reshape(blks * own_q, doc_count) * doc_weight[0][None, :]  1.92 us

profile of v2, /device:TPU:1, one launch (start us, length us, event | category | flops | bytes accessed | tf_op | source)
XLA Modules:
  0.0 56.6 jit_solution(13892351994101393712)
XLA Ops:
  0.0 54.0 %shard_map.67 = f32[8,2,16,256]{3,2,1,0:T(8,128)} custom-call(bf16[256,2048]{1,0:T(8,128)(2,1)} %bitcast.5, s32[1,256]{1,0:T(1,128)} %bitcast.8, s32[1,256]{1,0:T(1,128)} %doc_ref.1, bf16[32,2048]{1,0:T(8,128)(2,1)} %query_hbm.1, bf16[32,2048]{1,0:T(8,128)(2,1)} %bitcast.7), custom_call_target="tpu_custom_call" | custom-call | tf_op jit(solution)/shard_map/pallas_call | solution.py:230
  54.0 0.0 copy-start
  54.0 0.7 %copy-done = f32[1,256]{1,0:T(1,128)S(1)} copy-done((f32[1,256]{1,0:T(1,128)S(1)}, f32[1,256]{1,0:T(1,128)}, u32[]{:S(2)}) %copy-start) | copy-done | bytes 1048
  54.6 1.9 %copy_multiply_fusion = f32[256,1,256]{2,1,0:T(1,128)} fusion(f32[256,1,256]{2,0,1:T(8,128)} %bitcast.6, f32[256]{0:T(256)S(1)} %bitcast.9), kind=kLoop, calls=%fused_computation | loop fusion | flops 65536 | bytes 525312 | tf_op jit(solution)/shard_map/mul | solution.py:261
Async XLA Ops:
  54.0 0.7 %copy-start = (f32[1,256]{1,0:T(1,128)S(1)}, f32[1,256]{1,0:T(1,128)}, u32[]{:S(2)}) copy-start(f32[1,256]{1,0:T(1,128)} %param.9) | copy-start | bytes 3076

commit v3 on v1

v3 whole, which is shorter than its diff:
```python
import jax
import jax.numpy as jnp
from jax import lax
from jax.experimental import pallas as pl
from jax.experimental.pallas import tpu as pltpu
from jax.sharding import PartitionSpec as P

X, Y, Z_LO, Z_HI = 4, 4, 8, 2
MESH = pl.DeviceIdType.MESH
NN = (((1,), (0,)), ((), ()))
NT = (((1,), (1,)), ((), ()))
TN = (((0,), (0,)), ((), ()))
F32, BF16 = jnp.float32, jnp.bfloat16


def dot(a, b, dims):
    return lax.dot_general(a, b, dims, preferred_element_type=F32)


def iota(shape, axis):
    return lax.broadcasted_iota(jnp.int32, shape, axis)


def kernel(
    rows_hbm, owner_hbm, doc_hbm, weight_hbm, query_hbm, pre_hbm, out_ref,
    rows, owner, doc, weight, query, pre, mine, tiles, gathered, pick,
    id_send, id_got, send, got,
    loc_sem, go_sem, sw_s, sw_r, z_s, z_r, x_s, x_r, y_s, y_r, p_s, p_r,
    i_s, i_r, a_s, a_r,
):
    chips = X * Z_LO
    count = rows.shape[1]
    owners = 2 * chips
    cap = 2 * count // owners
    d, b = lax.axis_index("docs"), lax.axis_index("blk")
    core, chip = d % 2, d // 2
    x, z_lo = chip // Z_LO, chip % Z_LO
    y, z_hi = b // Z_HI, b % Z_HI
    native = core == z_hi
    low = z_hi == 0

    def at(dx=0, dy=0, lo=None, hi=None, c=None):
        lo, hi, c = (z_lo if lo is None else lo), (z_hi if hi is None else hi), (core if c is None else c)
        return {"docs": ((x + dx) % X * Z_LO + lo) * 2 + c, "blk": (y + dy) % Y * Z_HI + hi}

    def remote(src, dst, s, r, device):
        return pltpu.make_async_remote_copy(
            src_ref=src, dst_ref=dst, send_sem=s, recv_sem=r, device_id=device, device_id_type=MESH
        )

    barrier = pltpu.get_barrier_semaphore()

    def greet(device):
        pl.semaphore_signal(barrier, inc=1, device_id=device, device_id_type=MESH)

    for j in range(1, X):
        greet(at(dx=j))
    for j in range(1, Y):
        greet(at(dy=j))
    partner = at(c=1 - core)

    @pl.when(native)
    def _():
        greet(partner)
        for o in range(1, Z_LO):
            for c in range(2):
                greet(at(lo=(z_lo + o) % Z_LO, c=c))

    @pl.when(jnp.logical_not(native))
    def _():
        greet(partner)

    @pl.when(jnp.logical_and(low, native))
    def _():
        greet(at(hi=1))

    @pl.when(jnp.logical_and(low, jnp.logical_not(native)))
    def _():
        for o in range(Z_LO):
            for c in range(2):
                greet(at(lo=(z_lo + o) % Z_LO, hi=1, c=c))

    loads = [
        pltpu.make_async_copy(src, dst, loc_sem.at[i])
        for i, (src, dst) in enumerate(
            [
                (query_hbm, query), (pre_hbm, pre), (rows_hbm, rows.at[core]),
                (owner_hbm, owner.at[core]), (doc_hbm, doc.at[core]), (weight_hbm, weight),
            ]
        )
    ]
    for copy in loads:
        copy.start()

    loads[0].wait()
    loads[1].wait()
    block = dot(query[...], jnp.concatenate([pre[...]] * 4, axis=0), NT)
    group = iota((8, 128), 1) // 32
    tile = jnp.zeros((8, 128), F32)
    for j in range(4):
        tile = jnp.where(group == j, block[8 * j:8 * j + 8], tile)
    tile = tile.astype(BF16)
    mine[...] = tile

    def place(lo, c):
        return tiles.at[lo % 2 * 2 + c, lo // 2]

    @pl.when(native)
    def _():
        tiles[z_lo % 2 * 2 + core, z_lo // 2] = tile

    few = 2 * X + 2 * Y - 2 - (X + Y) + Z_LO
    many = few + Z_LO
    pl.semaphore_wait(barrier, jnp.where(low, few, many + jnp.where(native, 0, 1)))

    def tile_copy(o, hi, c=None):
        return remote(
            mine, place(z_lo, core), z_s.at[hi, o], z_r.at[o, core], at(lo=(z_lo + o) % Z_LO, hi=hi, c=z_hi)
        )

    def tile_wait(o, c):
        remote(mine, place((z_lo - o + Z_LO) % Z_LO, c), z_s.at[0, 0], z_r.at[o, c], partner).wait_recv()

    high = jnp.logical_not(low)

    @pl.when(high)
    def _():
        for o in range(Z_LO):
            tile_copy(o, 0).start()

    for o in range(Z_LO - 1, 0, -1):
        tile_copy(o, z_hi).start()

    @pl.when(jnp.logical_not(native))
    def _():
        tile_copy(0, z_hi).start()

    def go(device):
        pl.semaphore_signal(go_sem, inc=1, device_id=device, device_id_type=MESH)

    @pl.when(jnp.logical_and(high, jnp.logical_not(native)))
    def _():
        go(at(hi=0))

    loads[3].wait()
    loads[4].wait()
    swaps = [
        remote(owner.at[core], owner.at[core], sw_s.at[0], sw_r.at[0], partner),
        remote(doc.at[core], doc.at[core], sw_s.at[1], sw_r.at[1], partner),
        remote(rows_hbm, rows.at[core], sw_s.at[2], sw_r.at[2], partner),
    ]
    for copy in swaps:
        copy.start()

    swaps[0].wait()
    swaps[1].wait()
    before = (iota((count, count), 0) < iota((count, count), 1)).astype(BF16)
    id_table = jnp.zeros((owners, 128), F32)
    for side in range(2):
        owner_row = owner[side]
        table = iota((owners, count), 0) == owner_row
        earlier = dot(table.astype(BF16), before, NN)
        rank = jnp.sum(jnp.where(table, earlier, 0.0), axis=0, keepdims=True).astype(jnp.int32)
        slot = owner_row * cap + rank
        pick[side] = (iota((owners * cap, count), 0) == slot).astype(BF16)
        doc_side = jnp.where(table, (doc[side] + 1).astype(F32), 0.0).astype(BF16)
        lane_side = (iota((128, count), 0) == side * cap + rank).astype(BF16)
        id_table = id_table + dot(doc_side, lane_side, NT)
    id_send[...] = id_table.reshape(id_send.shape)
    n = 4 * 128
    row, col = iota((n, n), 0), iota((n, n), 1)
    turn = (row // 128 == col % 128 // 32) & (row % 128 // 32 == col // 128) & (row % 32 == col % 32)
    turn = turn.astype(BF16)

    own_piece = gathered.at[y, x]
    over = remote(own_piece, own_piece, p_s, p_r, at(hi=1))
    by_piece = jnp.logical_and(high, jnp.logical_not(native))

    @pl.when(by_piece)
    def _():
        over.wait_recv()

    @pl.when(jnp.logical_not(by_piece))
    def _():
        @pl.when(jnp.logical_not(native))
        def _():
            tile_wait(0, 0)
            tile_wait(0, 1)

        @pl.when(native)
        def _():
            tile_wait(0, 1 - core)

        for o in range(1, Z_LO):
            for c in range(2):
                tile_wait(o, c)
        left = [tiles[i].astype(F32).reshape(Z_LO // 2 * 8, 128).astype(BF16) for i in range(4)]
        mixed = dot(jnp.concatenate(left, axis=1), turn, NN)
        for p in range(Z_LO // 2):
            part = [mixed[8 * p:8 * p + 8, 128 * j:128 * j + 128] for j in range(4)]
            gathered[y, x, :, 128 * p:128 * p + 128] = jnp.concatenate(part, axis=0).astype(BF16)

    across, along = [], []
    for j in range(1, X):
        across.append(remote(own_piece, own_piece, x_s.at[j - 1], x_r.at[j - 1], at(dx=j)))
        across[-1].start()
    for i in range(X):
        if i:
            across[i - 1].wait_recv()
        piece = gathered.at[y, (x - i + X) % X]
        for j in range(1, Y):
            along.append(remote(piece, piece, y_s.at[j - 1, i], y_r.at[j - 1, i], at(dy=j)))
            along[-1].start()
        if i == min(1, X - 1):
            @pl.when(jnp.logical_and(low, native))
            def _():
                pl.semaphore_wait(go_sem, 1)
                over.start()

    def target(t):
        other = (chip + t // 2) % chips * 2 + t % 2
        return other, {"docs": other, "blk": b}

    def id_copy(t):
        other, device = target(t)
        return remote(id_send.at[other], id_got.at[chip], i_s.at[t], i_r.at[t // 2], device)

    def score_copy(t):
        other, device = target(t)
        return remote(send.at[other], got.at[core, chip], a_s.at[t], a_r.at[core, t // 2], device)

    def score_wait(c, i):
        remote(send.at[0], got.at[c, (chip - i + chips) % chips], a_s.at[0], a_r.at[c, i], partner).wait_recv()

    def loop(start, stop, fn):
        lax.fori_loop(start, stop, lambda i, c: (fn(i), c)[1], 0)

    own_ids = pltpu.make_async_copy(id_send.at[d], id_got.at[chip], loc_sem.at[6])

    @pl.when(native)
    def _():
        loop(2, owners, lambda t: id_copy(t).start())
        id_copy(1 - core).start()
        own_ids.start()

    loads[2].wait()
    swaps[2].wait()
    for copy in along:
        copy.wait_recv()

    span = gathered.shape[3]
    packed = []
    for side in range(2):
        part = None
        for i in range(X):
            term = dot(rows[side, :, i * span:(i + 1) * span], gathered[:, i].reshape(-1, span), NT)
            part = term if part is None else part + term
        packed.append(dot(pick[side], part.astype(BF16), NN).reshape(owners, cap, -1))
    send[...] = jnp.concatenate(packed, axis=1).astype(BF16)

    @pl.when(native)
    def _():
        own_ids.wait()

    @pl.when(jnp.logical_not(native))
    def _():
        id_copy(1 - core).wait_recv()

    loop(2, owners, lambda t: score_copy(t).start())
    score_copy(1 - core).start()
    own_scores = pltpu.make_async_copy(send.at[d], got.at[core, chip], loc_sem.at[7])
    own_scores.start()

    loop(1, chips, lambda i: id_copy(2 * i).wait_recv())
    per = chips * 2 * cap
    spread = (iota((per, chips), 0) // (2 * cap) == iota((per, chips), 1)).astype(BF16)
    ids = dot(spread, id_got[...].reshape(chips, 128).astype(BF16), NN)
    keep = iota(ids.shape, 1) == iota(ids.shape, 0) % (2 * cap)
    column = jnp.sum(jnp.where(keep, ids, 0.0), axis=1, keepdims=True).astype(jnp.int32) - 1
    member = (column == iota((per, weight.shape[1]), 1)).astype(BF16)
    loads[5].wait()

    own_scores.wait()
    for first in range(2):
        c = z_hi if first == 0 else 1 - z_hi

        @pl.when(c != core)
        def _():
            score_wait(c, 0)

        loop(1, chips, lambda i: score_wait(c, i))
        total = dot(got[c].reshape(per, -1), member, TN) * weight[...]
        size = total.shape[0] // Y
        for k in range(Y):
            for nh in range(2):
                out_ref[k, c, pl.ds(nh, size, stride=2), :] = total[k * size:(k + 1) * size, nh * 128:nh * 128 + 128]

    @pl.when(high)
    def _():
        for o in range(Z_LO):
            tile_copy(o, 0).wait_send()

    for o in range(1, Z_LO):
        tile_copy(o, z_hi).wait_send()

    @pl.when(jnp.logical_not(native))
    def _():
        tile_copy(0, z_hi).wait_send()

    @pl.when(native)
    def _():
        loop(2, owners, lambda t: id_copy(t).wait_send())
        id_copy(1 - core).wait_send()

    @pl.when(jnp.logical_and(low, native))
    def _():
        over.wait_send()

    for copy in across + along:
        copy.wait_send()
    loop(2, owners, lambda t: score_copy(t).wait_send())
    score_copy(1 - core).wait_send()


def shards(group_rows, group_owner, group_doc, doc_weight, queries, precond):
    rows = group_rows[0]
    count, width = rows.shape
    docs, blks = lax.axis_size("docs"), lax.axis_size("blk")
    chips = X * Z_LO
    cap = 2 * count // docs
    own_q, part = queries.shape[0], precond.shape[1]
    doc_count = doc_weight.shape[1]
    dma = pltpu.SemaphoreType.DMA
    any_spec = pl.BlockSpec(memory_space=pl.ANY)
    vmem = pl.BlockSpec(memory_space=pltpu.VMEM)
    nx, ny = max(X - 1, 1), max(Y - 1, 1)
    total = pl.pallas_call(
        kernel,
        out_shape=jax.ShapeDtypeStruct((Y, 2, 2 * own_q, doc_count // 2), F32),
        in_specs=[any_spec] * 6,
        out_specs=vmem,
        scratch_shapes=[
            pltpu.VMEM((2, count, width), BF16),
            pltpu.VMEM((2, 1, count), jnp.int32),
            pltpu.VMEM((2, 1, count), jnp.int32),
            pltpu.VMEM((1, doc_count), F32),
            pltpu.VMEM(queries.shape, BF16),
            pltpu.VMEM((part, width), BF16),
            pltpu.VMEM((8, 128), BF16),
            pltpu.VMEM((4, Z_LO // 2, 8, 128), BF16),
            pltpu.VMEM((Y, X, own_q, width // X), BF16),
            pltpu.VMEM((2, docs * cap, count), BF16),
            pltpu.VMEM((docs, 1, 128), F32),
            pltpu.VMEM((chips, 1, 128), F32),
            pltpu.VMEM((docs, 2 * cap, Y * own_q), BF16),
            pltpu.VMEM((2, chips, 2 * cap, Y * own_q), BF16),
            dma((8,)), pltpu.SemaphoreType.REGULAR, dma((3,)), dma((3,)),
            dma((2, Z_LO)), dma((Z_LO, 2)), dma((nx,)), dma((nx,)), dma((ny, X)), dma((ny, X)), dma, dma,
            dma((docs,)), dma((chips,)), dma((docs,)), dma((2, chips)),
        ],
        compiler_params=pltpu.CompilerParams(collective_id=0, has_side_effects=True),
    )(rows, group_owner.reshape(1, count), group_doc, doc_weight, queries, precond.T)
    return total.reshape(blks * own_q, 1, doc_count)


def solution(mesh):
    return jax.shard_map(
        shards,
        mesh=mesh,
        in_specs=(
            P("blk", "docs", None),
            P("blk", "docs", None),
            P("blk", "docs"),
            P("blk", "docs"),
            P("blk", None),
            P(None, "docs"),
        ),
        out_specs=P(None, "blk", "docs"),
        check_vma=False,
    )
```

time: 259 us -> 53.7 us (0.21)
  blocking collectives: 129 us -> 0 us
  waiting for transfers between devices: 95.3 us -> 0 us
  Pallas kernels: 0 us -> 51.7 us
  between operations: 13.5 us -> 0.01 us
  starting transfers between devices: 11.4 us -> 0 us
  matrix products: 4.45 us -> 0 us
  local copies, waits for them, and re-layouts: 4.65 us -> 1.83 us
    all_gather x1 -> x0, blocking collectives: 129 us -> none  [shards(): full_rows = lax.all_gather(query_pre, 'docs', axis=1, tiled=True)]
    all_gather x1 -> x0, waiting for transfers between devices: 77.4 us -> none  [shards(): full = lax.all_gather(full_rows, 'blk', axis=0, tiled=True)]
    pallas_call x0 -> x1, Pallas kernels: none -> 51.7 us  [shards(): pl.pallas_call(kernel, out_shape=jax.ShapeDtypeStruct((Y, 2, 2 * own_q, d...]
    all_to_all x2 -> x0, waiting for transfers between devices: 17.9 us -> none  [the longest x1 17.9 us: shards(): got = lax.all_to_all(send, 'docs', split_axis=0, concat_axis=0, tiled=True)]
    all_to_all x2 -> x0, starting transfers between devices: 11.4 us -> none  [the longest x1 7.2 us: shards(): got = lax.all_to_all(send, 'docs', split_axis=0, concat_axis=0, tiled=True)]
    dot_general x4 -> x0, matrix products: 4.45 us -> none  [the longest x1 2.72 us: shards(): jnp.dot(pick.astype(jnp.bfloat16), part, preferred_element_type=jnp.float32)]
  transfers between devices with their start and end apart: 3 -> 0, of which waited for: 2 -> 0; matrix products, arithmetic and copies ran while one was open for 2% -> 0% of each run, Pallas kernels for 0% -> 0%
where the time goes in v3:
time: 53.7 us; the launch traced here: 53.5 us
  Pallas kernels  51.7 us (96%)
  local copies, waits for them, and re-layouts  1.83 us (3%)
    pallas_call x1, Pallas kernels, shards(): pl.pallas_call(kernel, out_shape=jax.ShapeDtypeStruct((Y, 2, 2 * own_q, d...  51.7 us
    unnamed x1, local copies, waits for them, and re-layouts  1.83 us

profile of v3, /device:TPU:1, one launch (start us, length us, event | category | flops | bytes accessed | tf_op | source)
XLA Modules:
  0.0 53.5 jit_solution(17132602009271436572)
XLA Ops:
  0.0 51.7 %shard_map.64 = f32[4,2,64,128]{3,2,1,0:T(8,128)} custom-call(bf16[256,2048]{1,0:T(8,128)(2,1)} %bitcast.4, s32[1,256]{1,0:T(1,128)} %bitcast.7, s32[1,256]{1,0:T(1,128)} %doc_hbm.1, f32[1,256]{1,0:T(1,128)} %weight_hbm.1, bf16[32,2048]{1,0:T(8,128)(2,1)} %query_hbm.1, bf16[32,2048]{1,0:T(8,128)(2,1)} %bitcast.6), custom_call_target="tpu_custom_call" | custom-call | tf_op jit(solution)/shard_map/pallas_call | solution.py:337
  51.7 1.8 %copy.9 = f32[256,1,256]{2,1,0:T(1,128)} copy(f32[256,1,256]{2,1,0:T(1,128)} %bitcast.5) | data formatting | bytes 524288

commit v4 on v3

--- a/solution.py
+++ b/solution.py
@@ -24,8 +24,8 @@
 def kernel(
     rows_hbm, owner_hbm, doc_hbm, weight_hbm, query_hbm, pre_hbm, out_ref,
     rows, owner, doc, weight, query, pre, mine, tiles, gathered, pick,
-    id_send, id_got, send, got,
-    loc_sem, go_sem, sw_s, sw_r, z_s, z_r, x_s, x_r, y_s, y_r, p_s, p_r,
+    id_send, id_got, send, got, before, turn,
+    loc_sem, go_sem, sw_s, sw_r, z_s, z_r, f_s, f_r, g_s, g_r, p_s, p_r,
     i_s, i_r, a_s, a_r,
 ):
     chips = X * Z_LO
@@ -92,6 +92,12 @@
     for copy in loads:
         copy.start()
 
+    before[...] = (iota((count, count), 0) < iota((count, count), 1)).astype(BF16)
+    n = 4 * 128
+    row, col = iota((n, n), 0), iota((n, n), 1)
+    placed = (row // 128 == col % 128 // 32) & (row % 128 // 32 == col // 128) & (row % 32 == col % 32)
+    turn[...] = placed.astype(BF16)
+
     loads[0].wait()
     loads[1].wait()
     block = dot(query[...], jnp.concatenate([pre[...]] * 4, axis=0), NT)
@@ -154,12 +160,11 @@
 
     swaps[0].wait()
     swaps[1].wait()
-    before = (iota((count, count), 0) < iota((count, count), 1)).astype(BF16)
     id_table = jnp.zeros((owners, 128), F32)
     for side in range(2):
         owner_row = owner[side]
         table = iota((owners, count), 0) == owner_row
-        earlier = dot(table.astype(BF16), before, NN)
+        earlier = dot(table.astype(BF16), before[...], NN)
         rank = jnp.sum(jnp.where(table, earlier, 0.0), axis=0, keepdims=True).astype(jnp.int32)
         slot = owner_row * cap + rank
         pick[side] = (iota((owners * cap, count), 0) == slot).astype(BF16)
@@ -167,11 +172,6 @@
         lane_side = (iota((128, count), 0) == side * cap + rank).astype(BF16)
         id_table = id_table + dot(doc_side, lane_side, NT)
     id_send[...] = id_table.reshape(id_send.shape)
-    n = 4 * 128
-    row, col = iota((n, n), 0), iota((n, n), 1)
-    turn = (row // 128 == col % 128 // 32) & (row % 128 // 32 == col // 128) & (row % 32 == col % 32)
-    turn = turn.astype(BF16)
-
     own_piece = gathered.at[y, x]
     over = remote(own_piece, own_piece, p_s, p_r, at(hi=1))
     by_piece = jnp.logical_and(high, jnp.logical_not(native))
@@ -195,42 +195,82 @@
             for c in range(2):
                 tile_wait(o, c)
         left = [tiles[i].astype(F32).reshape(Z_LO // 2 * 8, 128).astype(BF16) for i in range(4)]
-        mixed = dot(jnp.concatenate(left, axis=1), turn, NN)
+        mixed = dot(jnp.concatenate(left, axis=1), turn[...], NN)
         for p in range(Z_LO // 2):
             part = [mixed[8 * p:8 * p + 8, 128 * j:128 * j + 128] for j in range(4)]
-            gathered[y, x, :, 128 * p:128 * p + 128] = jnp.concatenate(part, axis=0).astype(BF16)
-
-    across, along = [], []
-    for j in range(1, X):
-        across.append(remote(own_piece, own_piece, x_s.at[j - 1], x_r.at[j - 1], at(dx=j)))
-        across[-1].start()
-    for i in range(X):
-        if i:
-            across[i - 1].wait_recv()
-        piece = gathered.at[y, (x - i + X) % X]
-        for j in range(1, Y):
-            along.append(remote(piece, piece, y_s.at[j - 1, i], y_r.at[j - 1, i], at(dy=j)))
-            along[-1].start()
-        if i == min(1, X - 1):
+            for half in range(2):
+                both = jnp.concatenate(part[2 * half:2 * half + 2], axis=0)
+                gathered[y, x, half, :, 128 * p:128 * p + 128] = both.astype(BF16)
+
+    def piece(dx, dy, half):
+        return gathered.at[(y - dy + Y) % Y, (x - dx + X) % X, half]
+
+    sizes = ((X, Y), (Y, X))
+
+    def first_copy(half, j):
+        device = at(dx=j) if half == 0 else at(dy=j)
+        own = piece(0, 0, half)
+        return remote(own, own, f_s.at[half, j], f_r.at[half, j], device)
+
+    def second_copy(half, i, j):
+        part = piece(i, 0, half) if half == 0 else piece(0, i, half)
+        device = at(dy=j) if half == 0 else at(dx=j)
+        return remote(part, part, g_s.at[half, i, j], g_r.at[half, i, j], device)
+
+    copies = []
+
+    def begin(copy):
+        copy.start()
+        copies.append(copy)
+
+    for j in (2, 1, 3):
+        for half in range(2):
+            if j < sizes[half][0]:
+                begin(first_copy(half, j))
+    for i in (0, 1, 3, 2):
+        for half in range(2):
+            if i >= sizes[half][0]:
+                continue
+            if i:
+                first_copy(half, i).wait_recv()
+            for j in (2, 1, 3):
+                if j < sizes[half][1]:
+                    begin(second_copy(half, i, j))
+        if i == 0:
             @pl.when(jnp.logical_and(low, native))
             def _():
                 pl.semaphore_wait(go_sem, 1)
                 over.start()
 
     def target(t):
-        other = (chip + t // 2) % chips * 2 + t % 2
-        return other, {"docs": other, "blk": b}
-
-    def id_copy(t):
-        other, device = target(t)
-        return remote(id_send.at[other], id_got.at[chip], i_s.at[t], i_r.at[t // 2], device)
-
-    def score_copy(t):
-        other, device = target(t)
-        return remote(send.at[other], got.at[core, chip], a_s.at[t], a_r.at[core, t // 2], device)
+        dz, dx, e = t // (2 * X), t // 2 % X, t % 2
+        return ((x + dx) % X * Z_LO + dz) * 2 + e
+
+    def id_copy(other):
+        return remote(id_send.at[other], id_got.at[chip], i_s.at[other], i_r.at[chip], {"docs": other, "blk": b})
+
+    def id_wait(i):
+        remote(id_send.at[0], id_got.at[i], i_s.at[0], i_r.at[i], partner).wait_recv()
+
+    def score_copy(other):
+        return remote(
+            send.at[other], got.at[core, chip], a_s.at[other], a_r.at[core, chip], {"docs": other, "blk": b}
+        )
 
     def score_wait(c, i):
-        remote(send.at[0], got.at[c, (chip - i + chips) % chips], a_s.at[0], a_r.at[c, i], partner).wait_recv()
+        remote(send.at[0], got.at[c, i], a_s.at[0], a_r.at[c, i], partner).wait_recv()
+
+    def others(fn):
+        def step(t, carry):
+            other = target(t)
+
+            @pl.when(other != d)
+            def _():
+                fn(other)
+
+            return carry
+
+        lax.fori_loop(0, owners, step, 0)
 
     def loop(start, stop, fn):
         lax.fori_loop(start, stop, lambda i, c: (fn(i), c)[1], 0)
@@ -239,16 +279,17 @@
 
     @pl.when(native)
     def _():
-        loop(2, owners, lambda t: id_copy(t).start())
-        id_copy(1 - core).start()
+        others(lambda other: id_copy(other).start())
         own_ids.start()
 
     loads[2].wait()
     swaps[2].wait()
-    for copy in along:
-        copy.wait_recv()
-
-    span = gathered.shape[3]
+    for half in range(2):
+        for i in range(sizes[half][0]):
+            for j in range(1, sizes[half][1]):
+                second_copy(half, i, j).wait_recv()
+
+    span = gathered.shape[4]
     packed = []
     for side in range(2):
         part = None
@@ -264,14 +305,13 @@
 
     @pl.when(jnp.logical_not(native))
     def _():
-        id_copy(1 - core).wait_recv()
-
-    loop(2, owners, lambda t: score_copy(t).start())
-    score_copy(1 - core).start()
+        id_wait(chip)
+
+    others(lambda other: score_copy(other).start())
     own_scores = pltpu.make_async_copy(send.at[d], got.at[core, chip], loc_sem.at[7])
     own_scores.start()
 
-    loop(1, chips, lambda i: id_copy(2 * i).wait_recv())
+    loop(1, chips, lambda i: id_wait((chip + i) % chips))
     per = chips * 2 * cap
     spread = (iota((per, chips), 0) // (2 * cap) == iota((per, chips), 1)).astype(BF16)
     ids = dot(spread, id_got[...].reshape(chips, 128).astype(BF16), NN)
@@ -286,9 +326,9 @@
 
         @pl.when(c != core)
         def _():
-            score_wait(c, 0)
-
-        loop(1, chips, lambda i: score_wait(c, i))
+            score_wait(c, chip)
+
+        loop(1, chips, lambda i: score_wait(c, (chip + i) % chips))
         total = dot(got[c].reshape(per, -1), member, TN) * weight[...]
         size = total.shape[0] // Y
         for k in range(Y):
@@ -309,17 +349,15 @@
 
     @pl.when(native)
     def _():
-        loop(2, owners, lambda t: id_copy(t).wait_send())
-        id_copy(1 - core).wait_send()
+        others(lambda other: id_copy(other).wait_send())
 
     @pl.when(jnp.logical_and(low, native))
     def _():
         over.wait_send()
 
-    for copy in across + along:
+    for copy in copies:
         copy.wait_send()
-    loop(2, owners, lambda t: score_copy(t).wait_send())
-    score_copy(1 - core).wait_send()
+    others(lambda other: score_copy(other).wait_send())
 
 
 def shards(group_rows, group_owner, group_doc, doc_weight, queries, precond):
@@ -333,7 +371,7 @@
     dma = pltpu.SemaphoreType.DMA
     any_spec = pl.BlockSpec(memory_space=pl.ANY)
     vmem = pl.BlockSpec(memory_space=pltpu.VMEM)
-    nx, ny = max(X - 1, 1), max(Y - 1, 1)
+    nx = max(X, Y)
     total = pl.pallas_call(
         kernel,
         out_shape=jax.ShapeDtypeStruct((Y, 2, 2 * own_q, doc_count // 2), F32),
@@ -348,14 +386,16 @@
             pltpu.VMEM((part, width), BF16),
             pltpu.VMEM((8, 128), BF16),
             pltpu.VMEM((4, Z_LO // 2, 8, 128), BF16),
-            pltpu.VMEM((Y, X, own_q, width // X), BF16),
+            pltpu.VMEM((Y, X, 2, own_q // 2, width // X), BF16),
             pltpu.VMEM((2, docs * cap, count), BF16),
             pltpu.VMEM((docs, 1, 128), F32),
             pltpu.VMEM((chips, 1, 128), F32),
             pltpu.VMEM((docs, 2 * cap, Y * own_q), BF16),
             pltpu.VMEM((2, chips, 2 * cap, Y * own_q), BF16),
+            pltpu.VMEM((count, count), BF16),
+            pltpu.VMEM((512, 512), BF16),
             dma((8,)), pltpu.SemaphoreType.REGULAR, dma((3,)), dma((3,)),
-            dma((2, Z_LO)), dma((Z_LO, 2)), dma((nx,)), dma((nx,)), dma((ny, X)), dma((ny, X)), dma, dma,
+            dma((2, Z_LO)), dma((Z_LO, 2)), dma((2, nx)), dma((2, nx)), dma((2, nx, nx)), dma((2, nx, nx)), dma, dma,
             dma((docs,)), dma((chips,)), dma((docs,)), dma((2, chips)),
         ],
         compiler_params=pltpu.CompilerParams(collective_id=0, has_side_effects=True),

time: 53.7 us -> 50.9 us (0.948)
  the two profiles are of different devices: /device:TPU:1 before, /device:TPU:64 now
where the time goes in v4:
time: 50.9 us; the launch traced here: 50.7 us
  Pallas kernels  48.9 us (96%)
  local copies, waits for them, and re-layouts  1.83 us (4%)
    pallas_call x1, Pallas kernels, shards(): pl.pallas_call(kernel, out_shape=jax.ShapeDtypeStruct((Y, 2, 2 * own_q, d...  48.9 us
    unnamed x1, local copies, waits for them, and re-layouts  1.83 us

profile of v4, /device:TPU:64, one launch (start us, length us, event | category | flops | bytes accessed | tf_op | source)
XLA Modules:
  0.0 50.7 jit_solution(14159769929950189349)
XLA Ops:
  0.0 48.9 %shard_map.64 = f32[4,2,64,128]{3,2,1,0:T(8,128)} custom-call(bf16[256,2048]{1,0:T(8,128)(2,1)} %bitcast.4, s32[1,256]{1,0:T(1,128)} %bitcast.7, s32[1,256]{1,0:T(1,128)} %doc_hbm.1, f32[1,256]{1,0:T(1,128)} %weight_hbm.1, bf16[32,2048]{1,0:T(8,128)(2,1)} %query_hbm.1, bf16[32,2048]{1,0:T(8,128)(2,1)} %bitcast.6), custom_call_target="tpu_custom_call" | custom-call | tf_op jit(solution)/shard_map/pallas_call | solution.py:375
  48.9 1.8 %copy.9 = f32[256,1,256]{2,1,0:T(1,128)} copy(f32[256,1,256]{2,1,0:T(1,128)} %bitcast.5) | data formatting | bytes 524288

commit v5 on v4

--- a/solution.py
+++ b/solution.py
@@ -6,6 +6,7 @@
 from jax.sharding import PartitionSpec as P
 
 X, Y, Z_LO, Z_HI = 4, 4, 8, 2
+REACH = 4
 MESH = pl.DeviceIdType.MESH
 NN = (((1,), (0,)), ((), ()))
 NT = (((1,), (1,)), ((), ()))
@@ -25,7 +26,7 @@
     rows_hbm, owner_hbm, doc_hbm, weight_hbm, query_hbm, pre_hbm, out_ref,
     rows, owner, doc, weight, query, pre, mine, tiles, gathered, pick,
     id_send, id_got, send, got, before, turn,
-    loc_sem, go_sem, sw_s, sw_r, z_s, z_r, f_s, f_r, g_s, g_r, p_s, p_r,
+    loc_sem, go_sem, sw_s, sw_r, z_s, z_r, r_s, f_s, f_r, g_s, g_r, p_s, p_r,
     i_s, i_r, a_s, a_r,
 ):
     chips = X * Z_LO
@@ -59,12 +60,21 @@
         greet(at(dy=j))
     partner = at(c=1 - core)
 
+    def near(o):
+        lo = (z_lo + o) % Z_LO
+        gap = jnp.abs(lo - z_lo)
+        return lo, jnp.logical_or(low, gap <= REACH)
+
     @pl.when(native)
     def _():
         greet(partner)
         for o in range(1, Z_LO):
-            for c in range(2):
-                greet(at(lo=(z_lo + o) % Z_LO, c=c))
+            lo, close = near(o)
+
+            @pl.when(close)
+            def _():
+                for c in range(2):
+                    greet(at(lo=lo, c=c))
 
     @pl.when(jnp.logical_not(native))
     def _():
@@ -117,7 +127,8 @@
 
     few = 2 * X + 2 * Y - 2 - (X + Y) + Z_LO
     many = few + Z_LO
-    pl.semaphore_wait(barrier, jnp.where(low, few, many + jnp.where(native, 0, 1)))
+    beyond = jnp.maximum(0, jnp.maximum(Z_LO - 1 - REACH - z_lo, z_lo - REACH))
+    pl.semaphore_wait(barrier, jnp.where(low, few, many - beyond + jnp.where(native, 0, 1)))
 
     def tile_copy(o, hi, c=None):
         return remote(
@@ -128,6 +139,25 @@
         remote(mine, place((z_lo - o + Z_LO) % Z_LO, c), z_s.at[0, 0], z_r.at[o, c], partner).wait_recv()
 
     high = jnp.logical_not(low)
+    first_side = z_lo < Z_LO - REACH
+
+    def passed(o):
+        lo = (z_lo - o + Z_LO) % Z_LO
+        on = jnp.where(first_side, lo < z_lo, jnp.logical_and(z_lo >= REACH, lo > z_lo))
+        return jnp.logical_and(jnp.logical_and(high, native), on)
+
+    def passing(fn):
+        goal = jnp.where(first_side, z_lo + REACH, jnp.maximum(z_lo - REACH, 0))
+        for o in range(1, Z_LO):
+            lo = (z_lo - o + Z_LO) % Z_LO
+
+            @pl.when(passed(o))
+            def _():
+                for c in range(2):
+                    tile = place(lo, c)
+                    away = (goal - lo + Z_LO) % Z_LO
+                    fn(remote(tile, tile, r_s.at[o, c], z_r.at[away, c], at(lo=goal)), o, c)
+
 
     @pl.when(high)
     def _():
@@ -135,7 +165,9 @@
             tile_copy(o, 0).start()
 
     for o in range(Z_LO - 1, 0, -1):
-        tile_copy(o, z_hi).start()
+        @pl.when(near(o)[1])
+        def _():
+            tile_copy(o, z_hi).start()
 
     @pl.when(jnp.logical_not(native))
     def _():
@@ -166,8 +198,8 @@
         table = iota((owners, count), 0) == owner_row
         earlier = dot(table.astype(BF16), before[...], NN)
         rank = jnp.sum(jnp.where(table, earlier, 0.0), axis=0, keepdims=True).astype(jnp.int32)
-        slot = owner_row * cap + rank
-        pick[side] = (iota((owners * cap, count), 0) == slot).astype(BF16)
+        slot = (owner_row * 2 + side) * cap + rank
+        pick[:, side * count:(side + 1) * count] = (iota((owners * 2 * cap, count), 0) == slot).astype(BF16)
         doc_side = jnp.where(table, (doc[side] + 1).astype(F32), 0.0).astype(BF16)
         lane_side = (iota((128, count), 0) == side * cap + rank).astype(BF16)
         id_table = id_table + dot(doc_side, lane_side, NT)
@@ -191,9 +223,19 @@
         def _():
             tile_wait(0, 1 - core)
 
+        @pl.when(jnp.logical_and(high, native))
+        def _():
+            def forward(copy, o, c):
+                tile_wait(o, c)
+                copy.start()
+
+            passing(forward)
+
         for o in range(1, Z_LO):
-            for c in range(2):
-                tile_wait(o, c)
+            @pl.when(jnp.logical_not(passed(o)))
+            def _():
+                for c in range(2):
+                    tile_wait(o, c)
         left = [tiles[i].astype(F32).reshape(Z_LO // 2 * 8, 128).astype(BF16) for i in range(4)]
         mixed = dot(jnp.concatenate(left, axis=1), turn[...], NN)
         for p in range(Z_LO // 2):
@@ -244,7 +286,8 @@
 
     def target(t):
         dz, dx, e = t // (2 * X), t // 2 % X, t % 2
-        return ((x + dx) % X * Z_LO + dz) * 2 + e
+        to = dz
+        return ((x + dx) % X * Z_LO + to) * 2 + e
 
     def id_copy(other):
         return remote(id_send.at[other], id_got.at[chip], i_s.at[other], i_r.at[chip], {"docs": other, "blk": b})
@@ -290,14 +333,9 @@
                 second_copy(half, i, j).wait_recv()
 
     span = gathered.shape[4]
-    packed = []
-    for side in range(2):
-        part = None
-        for i in range(X):
-            term = dot(rows[side, :, i * span:(i + 1) * span], gathered[:, i].reshape(-1, span), NT)
-            part = term if part is None else part + term
-        packed.append(dot(pick[side], part.astype(BF16), NN).reshape(owners, cap, -1))
-    send[...] = jnp.concatenate(packed, axis=1).astype(BF16)
+    full = jnp.concatenate([gathered[:, i].reshape(-1, span) for i in range(X)], axis=1)
+    part = jnp.concatenate([dot(rows[side], full, NT).astype(BF16) for side in range(2)], axis=0)
+    send[...] = dot(pick[...], part, NN).astype(BF16).reshape(send.shape)
 
     @pl.when(native)
     def _():
@@ -341,7 +379,13 @@
             tile_copy(o, 0).wait_send()
 
     for o in range(1, Z_LO):
-        tile_copy(o, z_hi).wait_send()
+        @pl.when(near(o)[1])
+        def _():
+            tile_copy(o, z_hi).wait_send()
+
+    @pl.when(jnp.logical_and(high, native))
+    def _():
+        passing(lambda copy, o, c: copy.wait_send())
 
     @pl.when(jnp.logical_not(native))
     def _():
@@ -374,7 +418,7 @@
     nx = max(X, Y)
     total = pl.pallas_call(
         kernel,
-        out_shape=jax.ShapeDtypeStruct((Y, 2, 2 * own_q, doc_count // 2), F32),
+        out_shape=pltpu.VMEM((Y, 2, 2 * own_q, doc_count // 2), F32),
         in_specs=[any_spec] * 6,
         out_specs=vmem,
         scratch_shapes=[
@@ -387,7 +431,7 @@
             pltpu.VMEM((8, 128), BF16),
             pltpu.VMEM((4, Z_LO // 2, 8, 128), BF16),
             pltpu.VMEM((Y, X, 2, own_q // 2, width // X), BF16),
-            pltpu.VMEM((2, docs * cap, count), BF16),
+            pltpu.VMEM((docs * 2 * cap, 2 * count), BF16),
             pltpu.VMEM((docs, 1, 128), F32),
             pltpu.VMEM((chips, 1, 128), F32),
             pltpu.VMEM((docs, 2 * cap, Y * own_q), BF16),
@@ -395,7 +439,7 @@
             pltpu.VMEM((count, count), BF16),
             pltpu.VMEM((512, 512), BF16),
             dma((8,)), pltpu.SemaphoreType.REGULAR, dma((3,)), dma((3,)),
-            dma((2, Z_LO)), dma((Z_LO, 2)), dma((2, nx)), dma((2, nx)), dma((2, nx, nx)), dma((2, nx, nx)), dma, dma,
+            dma((2, Z_LO)), dma((Z_LO, 2)), dma((Z_LO, 2)), dma((2, nx)), dma((2, nx)), dma((2, nx, nx)), dma((2, nx, nx)), dma, dma,
             dma((docs,)), dma((chips,)), dma((docs,)), dma((2, chips)),
         ],
         compiler_params=pltpu.CompilerParams(collective_id=0, has_side_effects=True),

time: 50.9 us -> 49.5 us (0.972)
  local copies, waits for them, and re-layouts: 1.83 us -> 0.71 us
    unnamed x1, local copies, waits for them, and re-layouts: 1.83 us -> 0.71 us
where the time goes in v5:
time: 49.5 us; the launch traced here: 49.4 us
  Pallas kernels  48.6 us (98%)
  local copies, waits for them, and re-layouts  0.71 us (1%)
    pallas_call x1, Pallas kernels, shards(): pl.pallas_call(kernel, out_shape=pltpu.VMEM((Y, 2, 2 * own_q, doc_count /...  48.6 us

profile of v5, /device:TPU:64, one launch (start us, length us, event | category | flops | bytes accessed | tf_op | source)
XLA Modules:
  0.0 49.4 jit_solution(8699009122228788441)
XLA Ops:
  0.0 48.6 %shard_map.64 = f32[4,2,64,128]{3,2,1,0:T(8,128)S(1)} custom-call(bf16[256,2048]{1,0:T(8,128)(2,1)} %bitcast.5, s32[1,256]{1,0:T(1,128)} %bitcast.7, s32[1,256]{1,0:T(1,128)} %doc_hbm.1, f32[1,256]{1,0:T(1,128)} %weight_hbm.1, bf16[32,2048]{1,0:T(8,128)(2,1)} %query_hbm.1, bf16[32,2048]{1,0:T(8,128)(2,1)} %bitcast.6), custom_call_target="tpu_custom_call" | custom-call | tf_op jit(solution)/shard_map/pallas_call | solution.py:419
  48.6 0.7 %copy.9 = f32[256,1,256]{2,1,0:T(1,128)} copy(f32[256,1,256]{2,1,0:T(1,128)S(1)} %bitcast.4) | data formatting | bytes 524288

commit v6 on v5

--- a/solution.py
+++ b/solution.py
@@ -62,8 +62,7 @@
 
     def near(o):
         lo = (z_lo + o) % Z_LO
-        gap = jnp.abs(lo - z_lo)
-        return lo, jnp.logical_or(low, gap <= REACH)
+        return lo, jnp.abs(lo - z_lo) <= REACH
 
     @pl.when(native)
     def _():
@@ -128,7 +127,7 @@
     few = 2 * X + 2 * Y - 2 - (X + Y) + Z_LO
     many = few + Z_LO
     beyond = jnp.maximum(0, jnp.maximum(Z_LO - 1 - REACH - z_lo, z_lo - REACH))
-    pl.semaphore_wait(barrier, jnp.where(low, few, many - beyond + jnp.where(native, 0, 1)))
+    pl.semaphore_wait(barrier, jnp.where(low, few, many + jnp.where(native, 0, 1)) - beyond)
 
     def tile_copy(o, hi, c=None):
         return remote(
@@ -144,7 +143,7 @@
     def passed(o):
         lo = (z_lo - o + Z_LO) % Z_LO
         on = jnp.where(first_side, lo < z_lo, jnp.logical_and(z_lo >= REACH, lo > z_lo))
-        return jnp.logical_and(jnp.logical_and(high, native), on)
+        return jnp.logical_and(native, on)
 
     def passing(fn):
         goal = jnp.where(first_side, z_lo + REACH, jnp.maximum(z_lo - REACH, 0))
@@ -223,7 +222,7 @@
         def _():
             tile_wait(0, 1 - core)
 
-        @pl.when(jnp.logical_and(high, native))
+        @pl.when(native)
         def _():
             def forward(copy, o, c):
                 tile_wait(o, c)
@@ -290,24 +289,24 @@
         return ((x + dx) % X * Z_LO + to) * 2 + e
 
     def id_copy(other):
-        return remote(id_send.at[other], id_got.at[chip], i_s.at[other], i_r.at[chip], {"docs": other, "blk": b})
-
-    def id_wait(i):
-        remote(id_send.at[0], id_got.at[i], i_s.at[0], i_r.at[i], partner).wait_recv()
+        return remote(id_send.at[other], id_got.at[chip], i_s, i_r.at[0], {"docs": other, "blk": b})
+
+    mate = d + 1 - 2 * core
+    mate_ids = remote(id_send.at[mate], id_got.at[chip], i_s, i_r.at[1], partner)
 
     def score_copy(other):
         return remote(
-            send.at[other], got.at[core, chip], a_s.at[other], a_r.at[core, chip], {"docs": other, "blk": b}
+            send.at[other], got.at[core, chip], a_s, a_r.at[core], {"docs": other, "blk": b}
         )
 
-    def score_wait(c, i):
-        remote(send.at[0], got.at[c, i], a_s.at[0], a_r.at[c, i], partner).wait_recv()
+    def settle(ref, sem):
+        pltpu.make_async_copy(ref, ref, sem).wait()
 
     def others(fn):
         def step(t, carry):
             other = target(t)
 
-            @pl.when(other != d)
+            @pl.when(other // 2 != chip)
             def _():
                 fn(other)
 
@@ -315,26 +314,31 @@
 
         lax.fori_loop(0, owners, step, 0)
 
-    def loop(start, stop, fn):
-        lax.fori_loop(start, stop, lambda i, c: (fn(i), c)[1], 0)
-
     own_ids = pltpu.make_async_copy(id_send.at[d], id_got.at[chip], loc_sem.at[6])
 
     @pl.when(native)
     def _():
         others(lambda other: id_copy(other).start())
+        mate_ids.start()
         own_ids.start()
 
     loads[2].wait()
     swaps[2].wait()
-    for half in range(2):
-        for i in range(sizes[half][0]):
-            for j in range(1, sizes[half][1]):
-                second_copy(half, i, j).wait_recv()
-
     span = gathered.shape[4]
-    full = jnp.concatenate([gathered[:, i].reshape(-1, span) for i in range(X)], axis=1)
-    part = jnp.concatenate([dot(rows[side], full, NT).astype(BF16) for side in range(2)], axis=0)
+    sums = [None, None]
+    for i in (0, 1, 3, 2):
+        if i >= X:
+            continue
+        for j in range(1, Y):
+            second_copy(0, i, j).wait_recv()
+        for j in range(Y if i else 0):
+            second_copy(1, j, i).wait_recv()
+        at_x = (x - i + X) % X
+        right = gathered[:, at_x].reshape(-1, span)
+        for side in range(2):
+            term = dot(rows[side, :, pl.ds(pl.multiple_of(at_x * span, span), span)], right, NT)
+            sums[side] = term if sums[side] is None else sums[side] + term
+    part = jnp.concatenate([total.astype(BF16) for total in sums], axis=0)
     send[...] = dot(pick[...], part, NN).astype(BF16).reshape(send.shape)
 
     @pl.when(native)
@@ -343,13 +347,14 @@
 
     @pl.when(jnp.logical_not(native))
     def _():
-        id_wait(chip)
+        mate_ids.wait_recv()
 
     others(lambda other: score_copy(other).start())
-    own_scores = pltpu.make_async_copy(send.at[d], got.at[core, chip], loc_sem.at[7])
+    score_copy(mate).start()
+    own_scores = pltpu.make_async_copy(send.at[d], got.at[core, chip], a_r.at[core])
     own_scores.start()
 
-    loop(1, chips, lambda i: id_wait((chip + i) % chips))
+    settle(id_got.at[pl.ds(0, chips - 1)], i_r.at[0])
     per = chips * 2 * cap
     spread = (iota((per, chips), 0) // (2 * cap) == iota((per, chips), 1)).astype(BF16)
     ids = dot(spread, id_got[...].reshape(chips, 128).astype(BF16), NN)
@@ -358,50 +363,44 @@
     member = (column == iota((per, weight.shape[1]), 1)).astype(BF16)
     loads[5].wait()
 
-    own_scores.wait()
+    @pl.when(high)
+    def _():
+        for o in range(Z_LO):
+            tile_copy(o, 0).wait_send()
+
+    for o in range(1, Z_LO):
+        @pl.when(near(o)[1])
+        def _():
+            tile_copy(o, z_hi).wait_send()
+
+    @pl.when(native)
+    def _():
+        passing(lambda copy, o, c: copy.wait_send())
+
+    @pl.when(jnp.logical_not(native))
+    def _():
+        tile_copy(0, z_hi).wait_send()
+
+    @pl.when(native)
+    def _():
+        settle(id_send.at[pl.ds(0, owners - 1)], i_s)
+
+    @pl.when(jnp.logical_and(low, native))
+    def _():
+        over.wait_send()
+
+    for copy in copies:
+        copy.wait_send()
     for first in range(2):
         c = z_hi if first == 0 else 1 - z_hi
-
-        @pl.when(c != core)
-        def _():
-            score_wait(c, chip)
-
-        loop(1, chips, lambda i: score_wait(c, (chip + i) % chips))
+        if first:
+            settle(send.at[pl.ds(0, owners - 1)], a_s)
+        settle(got.at[c], a_r.at[c])
         total = dot(got[c].reshape(per, -1), member, TN) * weight[...]
         size = total.shape[0] // Y
         for k in range(Y):
             for nh in range(2):
                 out_ref[k, c, pl.ds(nh, size, stride=2), :] = total[k * size:(k + 1) * size, nh * 128:nh * 128 + 128]
-
-    @pl.when(high)
-    def _():
-        for o in range(Z_LO):
-            tile_copy(o, 0).wait_send()
-
-    for o in range(1, Z_LO):
-        @pl.when(near(o)[1])
-        def _():
-            tile_copy(o, z_hi).wait_send()
-
-    @pl.when(jnp.logical_and(high, native))
-    def _():
-        passing(lambda copy, o, c: copy.wait_send())
-
-    @pl.when(jnp.logical_not(native))
-    def _():
-        tile_copy(0, z_hi).wait_send()
-
-    @pl.when(native)
-    def _():
-        others(lambda other: id_copy(other).wait_send())
-
-    @pl.when(jnp.logical_and(low, native))
-    def _():
-        over.wait_send()
-
-    for copy in copies:
-        copy.wait_send()
-    others(lambda other: score_copy(other).wait_send())
 
 
 def shards(group_rows, group_owner, group_doc, doc_weight, queries, precond):
@@ -438,9 +437,9 @@
             pltpu.VMEM((2, chips, 2 * cap, Y * own_q), BF16),
             pltpu.VMEM((count, count), BF16),
             pltpu.VMEM((512, 512), BF16),
-            dma((8,)), pltpu.SemaphoreType.REGULAR, dma((3,)), dma((3,)),
+            dma((7,)), pltpu.SemaphoreType.REGULAR, dma((3,)), dma((3,)),
             dma((2, Z_LO)), dma((Z_LO, 2)), dma((Z_LO, 2)), dma((2, nx)), dma((2, nx)), dma((2, nx, nx)), dma((2, nx, nx)), dma, dma,
-            dma((docs,)), dma((chips,)), dma((docs,)), dma((2, chips)),
+            dma, dma((2,)), dma, dma((2,)),
         ],
         compiler_params=pltpu.CompilerParams(collective_id=0, has_side_effects=True),
     )(rows, group_owner.reshape(1, count), group_doc, doc_weight, queries, precond.T)

time: 49.5 us -> 43.5 us (0.88)
  the two profiles are of different devices: /device:TPU:64 before, /device:TPU:1 now
where the time goes in v6:
time: 43.5 us; the launch traced here: 43.4 us
  Pallas kernels  42.7 us (98%)
  local copies, waits for them, and re-layouts  0.71 us (2%)
    pallas_call x1, Pallas kernels, shards(): pl.pallas_call(kernel, out_shape=pltpu.VMEM((Y, 2, 2 * own_q, doc_count /...  42.7 us

profile of v6, /device:TPU:1, one launch (start us, length us, event | category | flops | bytes accessed | tf_op | source)
XLA Modules:
  0.0 43.4 jit_solution(1428919310442510522)
XLA Ops:
  0.0 42.7 %shard_map.64 = f32[4,2,64,128]{3,2,1,0:T(8,128)S(1)} custom-call(bf16[256,2048]{1,0:T(8,128)(2,1)} %bitcast.5, s32[1,256]{1,0:T(1,128)} %bitcast.7, s32[1,256]{1,0:T(1,128)} %doc_hbm.1, f32[1,256]{1,0:T(1,128)} %weight_hbm.1, bf16[32,2048]{1,0:T(8,128)(2,1)} %query_hbm.1, bf16[32,2048]{1,0:T(8,128)(2,1)} %bitcast.6), custom_call_target="tpu_custom_call" | custom-call | tf_op jit(solution)/shard_map/pallas_call | solution.py:418
  42.7 0.7 %copy.9 = f32[256,1,256]{2,1,0:T(1,128)} copy(f32[256,1,256]{2,1,0:T(1,128)S(1)} %bitcast.4) | data formatting | bytes 524288

commit v7 on v6

--- a/solution.py
+++ b/solution.py
@@ -49,46 +49,6 @@
             src_ref=src, dst_ref=dst, send_sem=s, recv_sem=r, device_id=device, device_id_type=MESH
         )
 
-    barrier = pltpu.get_barrier_semaphore()
-
-    def greet(device):
-        pl.semaphore_signal(barrier, inc=1, device_id=device, device_id_type=MESH)
-
-    for j in range(1, X):
-        greet(at(dx=j))
-    for j in range(1, Y):
-        greet(at(dy=j))
-    partner = at(c=1 - core)
-
-    def near(o):
-        lo = (z_lo + o) % Z_LO
-        return lo, jnp.abs(lo - z_lo) <= REACH
-
-    @pl.when(native)
-    def _():
-        greet(partner)
-        for o in range(1, Z_LO):
-            lo, close = near(o)
-
-            @pl.when(close)
-            def _():
-                for c in range(2):
-                    greet(at(lo=lo, c=c))
-
-    @pl.when(jnp.logical_not(native))
-    def _():
-        greet(partner)
-
-    @pl.when(jnp.logical_and(low, native))
-    def _():
-        greet(at(hi=1))
-
-    @pl.when(jnp.logical_and(low, jnp.logical_not(native)))
-    def _():
-        for o in range(Z_LO):
-            for c in range(2):
-                greet(at(lo=(z_lo + o) % Z_LO, hi=1, c=c))
-
     loads = [
         pltpu.make_async_copy(src, dst, loc_sem.at[i])
         for i, (src, dst) in enumerate(
@@ -100,6 +60,48 @@
     ]
     for copy in loads:
         copy.start()
+
+    barrier = pltpu.get_barrier_semaphore()
+
+    def greet(device):
+        pl.semaphore_signal(barrier, inc=1, device_id=device, device_id_type=MESH)
+
+    partner = at(c=1 - core)
+
+    def near(o):
+        lo = (z_lo + o) % Z_LO
+        return lo, jnp.abs(lo - z_lo) <= REACH
+
+    @pl.when(native)
+    def _():
+        for o in range(1, Z_LO):
+            lo, close = near(o)
+
+            @pl.when(close)
+            def _():
+                for c in range(2):
+                    greet(at(lo=lo, c=c))
+
+        greet(partner)
+
+    @pl.when(jnp.logical_not(native))
+    def _():
+        greet(partner)
+
+    @pl.when(jnp.logical_and(low, native))
+    def _():
+        greet(at(hi=1))
+
+    @pl.when(jnp.logical_and(low, jnp.logical_not(native)))
+    def _():
+        for o in range(Z_LO):
+            for c in range(2):
+                greet(at(lo=(z_lo + o) % Z_LO, hi=1, c=c))
+
+    for j in range(1, X):
+        greet(at(dx=j))
+    for j in range(1, Y):
+        greet(at(dy=j))
 
     before[...] = (iota((count, count), 0) < iota((count, count), 1)).astype(BF16)
     n = 4 * 128
@@ -283,11 +285,6 @@
                 pl.semaphore_wait(go_sem, 1)
                 over.start()
 
-    def target(t):
-        dz, dx, e = t // (2 * X), t // 2 % X, t % 2
-        to = dz
-        return ((x + dx) % X * Z_LO + to) * 2 + e
-
     def id_copy(other):
         return remote(id_send.at[other], id_got.at[chip], i_s, i_r.at[0], {"docs": other, "blk": b})
 
@@ -302,17 +299,23 @@
     def settle(ref, sem):
         pltpu.make_async_copy(ref, ref, sem).wait()
 
+    columns = [(x + dx) % X * Z_LO * 2 for dx in range(X)]
+
     def others(fn):
-        def step(t, carry):
-            other = target(t)
-
-            @pl.when(other // 2 != chip)
+        def step(turn_no, carry):
+            to = turn_no % 2 * (Z_LO // 2) + turn_no // 2
+
+            @pl.when(to != z_lo)
             def _():
-                fn(other)
-
+                for e in range(2):
+                    fn(columns[0] + 2 * to + e)
+
+            for dx in range(1, X):
+                for e in range(2):
+                    fn(columns[dx] + 2 * to + e)
             return carry
 
-        lax.fori_loop(0, owners, step, 0)
+        lax.fori_loop(0, Z_LO, step, 0)
 
     own_ids = pltpu.make_async_copy(id_send.at[d], id_got.at[chip], loc_sem.at[6])
 

time: 43.5 us -> 43.1 us (level)
    pallas_call x1, Pallas kernels: 42.7 us -> 42.3 us  [shards(): pl.pallas_call(kernel, out_shape=pltpu.VMEM((Y, 2, 2 * own_q, doc_count /...]
where the time goes in v7:
time: 43.1 us; the launch traced here: 43 us
  Pallas kernels  42.3 us (98%)
  local copies, waits for them, and re-layouts  0.71 us (2%)
    pallas_call x1, Pallas kernels, shards(): pl.pallas_call(kernel, out_shape=pltpu.VMEM((Y, 2, 2 * own_q, doc_count /...  42.3 us

profile of v7, /device:TPU:1, one launch (start us, length us, event | category | flops | bytes accessed | tf_op | source)
XLA Modules:
  0.0 43.0 jit_solution(11757631212962187136)
XLA Ops:
  0.0 42.3 %shard_map.64 = f32[4,2,64,128]{3,2,1,0:T(8,128)S(1)} custom-call(bf16[256,2048]{1,0:T(8,128)(2,1)} %bitcast.5, s32[1,256]{1,0:T(1,128)} %bitcast.7, s32[1,256]{1,0:T(1,128)} %doc_hbm.1, f32[1,256]{1,0:T(1,128)} %weight_hbm.1, bf16[32,2048]{1,0:T(8,128)(2,1)} %query_hbm.1, bf16[32,2048]{1,0:T(8,128)(2,1)} %bitcast.6), custom_call_target="tpu_custom_call" | custom-call | tf_op jit(solution)/shard_map/pallas_call | solution.py:421
  42.3 0.7 %copy.9 = f32[256,1,256]{2,1,0:T(1,128)} copy(f32[256,1,256]{2,1,0:T(1,128)S(1)} %bitcast.4) | data formatting | bytes 524288

commit v8 on v7

--- a/solution.py
+++ b/solution.py
@@ -72,12 +72,16 @@
         lo = (z_lo + o) % Z_LO
         return lo, jnp.abs(lo - z_lo) <= REACH
 
+    def sends(o):
+        lo, close = near(o)
+        return jnp.logical_or(close, jnp.logical_and(low, lo < z_lo))
+
     @pl.when(native)
     def _():
         for o in range(1, Z_LO):
             lo, close = near(o)
 
-            @pl.when(close)
+            @pl.when(jnp.logical_or(close, jnp.logical_and(low, lo > z_lo)))
             def _():
                 for c in range(2):
                     greet(at(lo=lo, c=c))
@@ -128,7 +132,7 @@
 
     few = 2 * X + 2 * Y - 2 - (X + Y) + Z_LO
     many = few + Z_LO
-    beyond = jnp.maximum(0, jnp.maximum(Z_LO - 1 - REACH - z_lo, z_lo - REACH))
+    beyond = jnp.maximum(0, jnp.maximum(Z_LO - 1 - REACH - z_lo, jnp.where(low, 0, z_lo - REACH)))
     pl.semaphore_wait(barrier, jnp.where(low, few, many + jnp.where(native, 0, 1)) - beyond)
 
     def tile_copy(o, hi, c=None):
@@ -144,7 +148,7 @@
 
     def passed(o):
         lo = (z_lo - o + Z_LO) % Z_LO
-        on = jnp.where(first_side, lo < z_lo, jnp.logical_and(z_lo >= REACH, lo > z_lo))
+        on = jnp.where(first_side, lo < z_lo, jnp.logical_and(jnp.logical_and(high, z_lo >= REACH), lo > z_lo))
         return jnp.logical_and(native, on)
 
     def passing(fn):
@@ -166,7 +170,7 @@
             tile_copy(o, 0).start()
 
     for o in range(Z_LO - 1, 0, -1):
-        @pl.when(near(o)[1])
+        @pl.when(sends(o))
         def _():
             tile_copy(o, z_hi).start()
 
@@ -372,7 +376,7 @@
             tile_copy(o, 0).wait_send()
 
     for o in range(1, Z_LO):
-        @pl.when(near(o)[1])
+        @pl.when(sends(o))
         def _():
             tile_copy(o, z_hi).wait_send()
 

time: 43.1 us -> 43.2 us (level)
  no operation moved by 1% of the time
where the time goes in v8:
time: 43.2 us; the launch traced here: 43 us
  Pallas kernels  42.3 us (98%)
  local copies, waits for them, and re-layouts  0.71 us (2%)
    pallas_call x1, Pallas kernels, shards(): pl.pallas_call(kernel, out_shape=pltpu.VMEM((Y, 2, 2 * own_q, doc_count /...  42.3 us

profile of v8, /device:TPU:1, one launch (start us, length us, event | category | flops | bytes accessed | tf_op | source)
XLA Modules:
  0.0 43.0 jit_solution(6102526292883655257)
XLA Ops:
  0.0 42.3 %shard_map.64 = f32[4,2,64,128]{3,2,1,0:T(8,128)S(1)} custom-call(bf16[256,2048]{1,0:T(8,128)(2,1)} %bitcast.5, s32[1,256]{1,0:T(1,128)} %bitcast.7, s32[1,256]{1,0:T(1,128)} %doc_hbm.1, f32[1,256]{1,0:T(1,128)} %weight_hbm.1, bf16[32,2048]{1,0:T(8,128)(2,1)} %query_hbm.1, bf16[32,2048]{1,0:T(8,128)(2,1)} %bitcast.6), custom_call_target="tpu_custom_call" | custom-call | tf_op jit(solution)/shard_map/pallas_call | solution.py:425
  42.3 0.7 %copy.9 = f32[256,1,256]{2,1,0:T(1,128)} copy(f32[256,1,256]{2,1,0:T(1,128)S(1)} %bitcast.4) | data formatting | bytes 524288

commit v9 on v7

--- a/solution.py
+++ b/solution.py
@@ -321,8 +321,8 @@
 
     @pl.when(native)
     def _():
+        mate_ids.start()
         others(lambda other: id_copy(other).start())
-        mate_ids.start()
         own_ids.start()
 
     loads[2].wait()

time: 43.1 us -> 43.1 us (level)
  no operation moved by 1% of the time
where the time goes in v9:
time: 43.1 us; the launch traced here: 43 us
  Pallas kernels  42.3 us (98%)
  local copies, waits for them, and re-layouts  0.71 us (2%)
    pallas_call x1, Pallas kernels, shards(): pl.pallas_call(kernel, out_shape=pltpu.VMEM((Y, 2, 2 * own_q, doc_count /...  42.3 us

profile of v9, /device:TPU:1, one launch (start us, length us, event | category | flops | bytes accessed | tf_op | source)
XLA Modules:
  0.0 43.0 jit_solution(12096074349955791088)
XLA Ops:
  0.0 42.3 %shard_map.64 = f32[4,2,64,128]{3,2,1,0:T(8,128)S(1)} custom-call(bf16[256,2048]{1,0:T(8,128)(2,1)} %bitcast.5, s32[1,256]{1,0:T(1,128)} %bitcast.7, s32[1,256]{1,0:T(1,128)} %doc_hbm.1, f32[1,256]{1,0:T(1,128)} %weight_hbm.1, bf16[32,2048]{1,0:T(8,128)(2,1)} %query_hbm.1, bf16[32,2048]{1,0:T(8,128)(2,1)} %bitcast.6), custom_call_target="tpu_custom_call" | custom-call | tf_op jit(solution)/shard_map/pallas_call | solution.py:421
  42.3 0.7 %copy.9 = f32[256,1,256]{2,1,0:T(1,128)} copy(f32[256,1,256]{2,1,0:T(1,128)S(1)} %bitcast.4) | data formatting | bytes 524288
